TPU v7x, 32 devices: a whole 2x2x4 slice. The times are simulated.
32 devices in a mesh: gx: 8 (over y, x, core), gy: 4 (over z).
Axes of the slice: x: 2, y: 2, z: 4, core: 2. Of those that a mesh axis runs over, the one named last changes fastest.
Arguments:
- e_field: float32 [3, 3, 2048, 2048], P(None, None, 'gx', 'gy'), may hold values from -6 to 6
- h_field: float32 [3, 3, 2048, 2048], P(None, None, 'gx', 'gy'), may hold values from -6 to 6
- material: int32 [3, 2048, 2048], P(None, 'gx', 'gy'), may hold values from 0 to 7
- eps_table: float32 [8], replicated, may hold values from 1 to 12
- src_pos: int32 [1024, 3], replicated, may hold values from 0 to 2047, as said below
- src_amp: float32 [1024], replicated, may hold values from -40 to 40
- freqs: float32 [2], replicated, may hold values from 0.3 to 2.8
Outputs:
- e_out: float32 [3, 3, 2048, 2048], P(None, None, 'gx', 'gy')
- h_out: float32 [3, 3, 2048, 2048], P(None, None, 'gx', 'gy')
- far_field: float32 [1024, 8, 2, 1024], P('gx', None, None, 'gy')
Inputs may be any that keep to these rules, and one draw needn't show every extreme that they name: `src_pos`: each row is a cell (layer, row, column) of the slab; several sources may share a cell.
All inputs are finite; a program needn't handle non-finite values.
Results may differ from a plain program's by a relative error of at most 0.0054.
Values may be sent and summed in bfloat16 or wider, within the bound.
A program may use at most 192 MiB of HBM per device.

v0:
```python
import functools
import math

import jax
import jax.numpy as jnp
from jax import lax
from jax.experimental import pallas as pl
from jax.experimental.pallas import tpu as pltpu
from jax.sharding import PartitionSpec as P

LZ = 3
FACE = 1
STEPS = 2
NF = 2
NA = 1024
NMAT = 8

courant = 0.5
source_rate = 0.7
zoom_factor = 4

BASE = 32
CHUNK = 16
SETS = 2
EACH = 4 // SETS
PAD = 128
ANY = pl.BlockSpec(memory_space=pl.ANY)
VM = pl.BlockSpec(memory_space=pltpu.VMEM)
SM = pl.BlockSpec(memory_space=pltpu.SMEM)
BIG = 60 * 1024 * 1024


def shifted(block, axis, distance):
    size = lax.axis_size(axis)
    route = [(i - distance, i) for i in range(size) if 0 <= i - distance < size]
    return lax.ppermute(block, axis, route)


def yee_kernel(
    grid_rows, grid_cols, gx,
    e_hbm, h_hbm, m_hbm, colh, rowh, eps, pos, amp,
    e_out, h_out, *rest,
):
    sd_outs, (e_ext, h_ext, m_main, scale, src, first, sems) = rest[:SETS], rest[SETS:]
    rows, cols = m_main.shape[1:]
    width = cols + PAD
    high = e_ext.shape[1]
    row0 = lax.axis_index("gx") * rows
    col0 = lax.axis_index("gy") * cols
    main_r = pl.ds(BASE, rows)
    copies = [
        pltpu.make_async_copy(e_hbm, e_ext.at[:, main_r, pl.ds(0, cols)], sems.at[0]),
        pltpu.make_async_copy(h_hbm, h_ext.at[:, main_r, pl.ds(0, cols)], sems.at[1]),
        pltpu.make_async_copy(m_hbm, m_main, sems.at[2]),
    ]
    for copy in copies:
        copy.start()
    count = amp.shape[1]
    step = min(count, 1024)
    used = high - 2 * CHUNK
    row_at = row0 + lax.broadcasted_iota(jnp.int32, (used, step), 0) + (CHUNK - BASE)
    lane = lax.broadcasted_iota(jnp.int32, (width, step), 0)
    col_at = col0 + jnp.where(lane < cols + PAD // 2, lane, lane - width)
    for start in range(0, count, step):
        at = pl.ds(start, step)
        amp_now = amp[:, at]
        hi = amp_now.astype(jnp.bfloat16).astype(jnp.float32)
        mid = (amp_now - hi).astype(jnp.bfloat16).astype(jnp.float32)
        low = amp_now - hi - mid
        hit_col = jnp.where(col_at == pos[2:3, at], 1.0, 0.0).astype(jnp.bfloat16)
        hit_row = row_at == pos[1:2, at]
        for layer in range(LZ):
            hit = hit_row & (pos[0:1, at] == layer)
            total = None
            for piece in (hi, mid, low):
                left = jnp.where(hit, piece, 0.0).astype(jnp.bfloat16)
                term = lax.dot_general(
                    left, hit_col, (((1,), (1,)), ((), ())), preferred_element_type=jnp.float32
                )
                total = term if total is None else total + term
            if start == 0:
                src[layer, CHUNK : CHUNK + used, :] = total
            else:
                src[layer, CHUNK : CHUNK + used, :] += total
    copies[2].wait()

    def scale_of(index, row, col):
        value = jnp.full(index.shape, eps[0], jnp.float32)
        for material in range(1, NMAT):
            value = jnp.where(index == material, eps[material], value)
        inside = (row >= 0) & (row < grid_rows) & (col >= 0) & (col < grid_cols)
        return jnp.where(inside, courant / value, 0.0)

    col_main = col0 + lax.broadcasted_iota(jnp.int32, (CHUNK, cols), 1)
    lane_pad = lax.broadcasted_iota(jnp.int32, (CHUNK, PAD), 1)
    col_pad = col0 + jnp.where(lane_pad < PAD // 2, cols + lane_pad, lane_pad - PAD)
    row_chunk = row0 + lax.broadcasted_iota(jnp.int32, (CHUNK, cols), 0)

    def fill(step_index, carry):
        r = pl.multiple_of(step_index * CHUNK, CHUNK)
        near = pl.ds(r, CHUNK)
        far = pl.ds(BASE + r, CHUNK)
        for layer in range(LZ):
            scale[layer, far, :cols] = scale_of(m_main[layer, near, :], row_chunk + r, col_main)
            scale[layer, far, cols:] = scale_of(
                colh[6 * LZ + layer, near, :], row_chunk[:, :PAD] + r, col_pad
            )
        for plane in range(3 * LZ):
            e_ext[plane, far, cols:] = colh[plane, near, :]
            h_ext[plane, far, cols:] = colh[3 * LZ + plane, near, :]
        return carry

    lax.fori_loop(0, rows // CHUNK, fill, 0)
    lane_all = lax.broadcasted_iota(jnp.int32, (8, width), 1)
    col_all = col0 + jnp.where(lane_all < cols + PAD // 2, lane_all, lane_all - width)
    row_eight = row0 + lax.broadcasted_iota(jnp.int32, (8, width), 0)
    blank = jnp.zeros((8, width), jnp.float32)
    for place, target, offset, spare in (
        (0, BASE + rows, rows, BASE + rows + 8),
        (8, BASE - 8, -8, BASE - 16),
    ):
        for layer in range(LZ):
            scale[layer, target : target + 8, :] = scale_of(
                rowh[6 * LZ + layer, place : place + 8, :], row_eight + offset, col_all
            )
            scale[layer, spare : spare + 8, :] = blank
        for plane in range(3 * LZ):
            e_ext[plane, target : target + 8, :] = rowh[plane, place : place + 8, :]
            h_ext[plane, target : target + 8, :] = rowh[3 * LZ + plane, place : place + 8, :]
            e_ext[plane, spare : spare + 8, :] = blank
            h_ext[plane, spare : spare + 8, :] = blank
    for plane in range(3 * LZ):
        e_ext[plane, high - 16 : high, :] = jnp.zeros((16, width), jnp.float32)
        h_ext[plane, 0:16, :] = jnp.zeros((16, width), jnp.float32)
    lane_c = lax.broadcasted_iota(jnp.int32, (CHUNK, width), 1)
    col_c = col0 + jnp.where(lane_c < cols + PAD // 2, lane_c, lane_c - width)
    weight = jnp.where(col_c >= 0, courant, 0.0)
    top = lax.axis_index("gx") == 0
    copies[0].wait()
    copies[1].wait()

    def magnetic_pass(index, carry):
        r = pl.multiple_of(index * CHUNK, CHUNK)
        now = pl.ds(r, CHUNK)
        more = pl.ds(r, CHUNK + 8)
        factor = weight * jnp.where(top & (index * CHUNK < BASE), 0.0, 1.0)
        zero = jnp.zeros((CHUNK, width), jnp.float32)
        ex = [e_ext[layer, now, :] for layer in range(LZ)] + [zero]
        ey = [e_ext[LZ + layer, now, :] for layer in range(LZ)] + [zero]
        for layer in range(LZ):
            ez = e_ext[2 * LZ + layer, now, :]
            ez_row = pltpu.roll(e_ext[2 * LZ + layer, more, :], CHUNK + 7, 0)[:CHUNK]
            ey_row = pltpu.roll(e_ext[LZ + layer, more, :], CHUNK + 7, 0)[:CHUNK]
            ez_col = pltpu.roll(ez, width - 1, 1)
            ex_col = pltpu.roll(ex[layer], width - 1, 1)
            curl_x = ez_col - ez - (ey[layer + 1] - ey[layer])
            curl_y = ex[layer + 1] - ex[layer] - (ez_row - ez)
            curl_z = ey_row - ey[layer] - (ex_col - ex[layer])
            for part, curl in enumerate((curl_x, curl_y, curl_z)):
                plane = part * LZ + layer
                h_ext[plane, now, :] = h_ext[plane, now, :] - factor * curl
        return carry

    def electric_pass(moment, last, index, carry):
        r = pl.multiple_of(index * CHUNK, CHUNK)
        now = pl.ds(r, CHUNK)
        more = pl.ds(pl.multiple_of(r - 8, 8), CHUNK + 8)
        drive = math.sin(source_rate * moment)
        zero = jnp.zeros((CHUNK, width), jnp.float32)
        hx = [zero] + [h_ext[layer, now, :] for layer in range(LZ)]
        hy = [zero] + [h_ext[LZ + layer, now, :] for layer in range(LZ)]
        for layer in range(LZ):
            hz = h_ext[2 * LZ + layer, now, :]
            hz_row = pltpu.roll(h_ext[2 * LZ + layer, more, :], 1, 0)[8:]
            hy_row = pltpu.roll(h_ext[LZ + layer, more, :], 1, 0)[8:]
            hx_now, hy_now = hx[layer + 1], hy[layer + 1]
            hz_col = pltpu.roll(hz, 1, 1)
            hx_col = pltpu.roll(hx_now, 1, 1)
            curl_x = hz - hz_col - (hy_now - hy[layer])
            curl_y = hx_now - hx[layer] - (hz - hz_row)
            curl_z = hy_now - hy_row - (hx_now - hx_col)
            factor = scale[layer, now, :]
            new_x = e_ext[layer, now, :] + factor * curl_x
            new_y = e_ext[LZ + layer, now, :] + factor * curl_y
            new_z = e_ext[2 * LZ + layer, now, :] + factor * curl_z + drive * src[layer, now, :]
            e_ext[layer, now, :] = new_x
            e_ext[LZ + layer, now, :] = new_y
            e_ext[2 * LZ + layer, now, :] = new_z
            if layer == FACE:
                faces = (-hy_now, hx_now, new_y, -new_x)
                for item, face in enumerate(faces):
                    if last:
                        old = first[item, now, :]
                        here = pl.ds(r - BASE, CHUNK)
                        span = cols // gx
                        place = (item % EACH) * span
                        for which, value in enumerate((old + face, face - old)):
                            lo = which * EACH * span + place
                            for j in range(gx):
                                piece = value[:, j * span : (j + 1) * span].astype(jnp.bfloat16)
                                sd_outs[item // EACH][j, here, lo : lo + span] = piece
                    else:
                        first[item, now, :] = face
        return carry

    chunks = high // CHUNK
    main0 = BASE // CHUNK
    main1 = main0 + rows // CHUNK
    lax.fori_loop(1, chunks - 1, magnetic_pass, 0)
    lax.fori_loop(1, chunks - 1, functools.partial(electric_pass, 1.0, False), 0)
    lax.fori_loop(1, main1, magnetic_pass, 0)
    out_h = pltpu.make_async_copy(h_ext.at[:, main_r, pl.ds(0, cols)], h_out, sems.at[3])
    out_h.start()
    lax.fori_loop(main0, main1, functools.partial(electric_pass, 2.0, True), 0)
    out_e = pltpu.make_async_copy(e_ext.at[:, main_r, pl.ds(0, cols)], e_out, sems.at[4])
    out_e.start()
    out_h.wait()
    out_e.wait()


def yee(e_field, h_field, material, eps_table, src_pos, src_amp):
    rows, cols = material.shape[1:]
    gx = lax.axis_size("gx")
    grid_rows = rows * gx
    grid_cols = cols * lax.axis_size("gy")
    planes = 3 * LZ
    e = e_field.reshape(planes, rows, cols)
    h = h_field.reshape(planes, rows, cols)

    def edge(low, high, dim):
        cut = lambda a: lax.slice_in_dim(a, low, high, axis=dim)
        return jnp.concatenate([cut(e), cut(h), cut(material).astype(jnp.float32)], 0)

    send_prev = jnp.swapaxes(edge(0, 2, 2), 1, 2)
    send_next = jnp.swapaxes(edge(cols - 2, cols, 2), 1, 2)
    right = shifted(send_prev, "gy", -1)
    left = shifted(send_next, "gy", 1)
    right = jnp.swapaxes(right, 1, 2)
    left = jnp.swapaxes(left, 1, 2)
    total = 2 * planes + LZ
    col_halo = jnp.concatenate(
        [right, jnp.zeros((total, rows, PAD - 4), jnp.float32), left], 2
    )
    send_up = jnp.concatenate([edge(0, 2, 1), col_halo[:, 0:2]], 2)
    send_down = jnp.concatenate([edge(rows - 2, rows, 1), col_halo[:, rows - 2 :]], 2)
    below = shifted(send_up, "gx", -1)
    above = shifted(send_down, "gx", 1)
    row_halo = jnp.concatenate(
        [below, jnp.zeros((total, 12, cols + PAD), jnp.float32), above], 1
    )
    high = rows + 2 * BASE
    width = cols + PAD
    f32 = jnp.float32
    out = pl.pallas_call(
        functools.partial(yee_kernel, grid_rows, grid_cols, gx),
        out_shape=(
            jax.ShapeDtypeStruct((planes, rows, cols), f32),
            jax.ShapeDtypeStruct((planes, rows, cols), f32),
        )
        + (jax.ShapeDtypeStruct((gx, rows, 2 * EACH * (cols // gx)), jnp.bfloat16),) * SETS,
        in_specs=[ANY, ANY, ANY, VM, VM, SM, VM, VM],
        out_specs=(ANY, ANY) + (VM,) * SETS,
        scratch_shapes=[
            pltpu.VMEM((planes, high, width), f32),
            pltpu.VMEM((planes, high, width), f32),
            pltpu.VMEM((LZ, rows, cols), jnp.int32),
            pltpu.VMEM((LZ, high, width), f32),
            pltpu.VMEM((LZ, high, width), f32),
            pltpu.VMEM((4, high, width), f32),
            pltpu.SemaphoreType.DMA((5,)),
        ],
        compiler_params=pltpu.CompilerParams(vmem_limit_bytes=BIG),
        name="yee",
    )(
        e, h, material, col_halo, row_halo,
        eps_table, jnp.swapaxes(src_pos, 0, 1), src_amp[None, :],
    )
    return out


def table_kernel(a_re, a_im, b_re, b_im, out):
    lo_re, lo_im = b_re[...], b_im[...]
    for block in range(a_re.shape[1]):
        hi_re = a_re[:, block : block + 1]
        hi_im = a_im[:, block : block + 1]
        at = slice(block * 128, block * 128 + 128)
        out[0, 0, :, at] = (hi_re * lo_re - hi_im * lo_im).astype(jnp.bfloat16)
        out[0, 1, :, at] = (hi_re * lo_im + hi_im * lo_re).astype(jnp.bfloat16)


def unit(phase, period):
    angle = jnp.remainder(phase, period).astype(jnp.float32) * (2.0 * math.pi / period)
    return jnp.cos(angle), -jnp.sin(angle)


def table(row_index, first, length, period, blocks):
    count = row_index.shape[0]
    high = first + 128 * jnp.arange(length // 128, dtype=jnp.int32)
    low = jnp.arange(128, dtype=jnp.int32)
    a_re, a_im = unit(row_index[:, None] * high[None, :], period)
    b_re, b_im = unit(row_index[:, None] * low[None, :], period)
    size = count // blocks
    one = pl.BlockSpec((size, length // 128), lambda i: (i, 0))
    two = pl.BlockSpec((size, 128), lambda i: (i, 0))
    return pl.pallas_call(
        table_kernel,
        grid=(blocks,),
        out_shape=jax.ShapeDtypeStruct((blocks, 2, size, length), jnp.bfloat16),
        in_specs=[one, one, two, two],
        out_specs=pl.BlockSpec((1, 2, size, length), lambda i: (i, 0, 0, 0)),
        cost_estimate=pl.CostEstimate(
            flops=8 * count * length, bytes_accessed=4 * count * length, transcendentals=0
        ),
        name="chirp",
    )(a_re, a_im, b_re, b_im)


def rows_kernel(mix, tab, v, out):
    group, _, nu, depth = tab.shape
    half = v.shape[2] // 2
    left = tab[...].reshape(group * 2 * nu, depth)
    right = v[...].reshape(depth, 2 * half)
    both = jnp.dot(left, right, preferred_element_type=jnp.float32)
    both = both.reshape(group, 2, nu, 2 * half)
    for b in range(group):
        s_re, s_im = both[b, 0, :, :half], both[b, 1, :, :half]
        d_re, d_im = both[b, 0, :, half:], both[b, 1, :, half:]
        for f in range(NF):
            p_re, p_im, q_re, q_im = (mix[f, i] for i in range(4))
            re = p_re * s_re - p_im * s_im + (q_re * d_re - q_im * d_im)
            im = p_re * s_im + p_im * s_re + (q_re * d_im + q_im * d_re)
            out[b, f, 0] = re.astype(jnp.bfloat16)
            out[b, f, 1] = im.astype(jnp.bfloat16)


def cols_kernel(g, tab, out, left):
    gx, _, _, nu, wide = g.shape
    span = wide // EACH

    @pl.when(pl.program_id(0) == 0)
    def _():
        for f in range(NF):
            for c in range(2):
                got = [g[j, f, c].astype(jnp.float32) for j in range(gx)]
                for k in range(EACH):
                    at = (f * EACH + k) * nu
                    row = [piece[:, k * span : (k + 1) * span] for piece in got]
                    left[c, at : at + nu, :] = jnp.concatenate(row, 1).astype(jnp.bfloat16)

    y_re = tab[0, 0]
    y_im = tab[0, 1]
    dot = functools.partial(jnp.dot, preferred_element_type=jnp.float32)
    re = dot(left[0], y_re) - dot(left[1], y_im)
    im = dot(left[0], y_im) + dot(left[1], y_re)
    for i in range(NF * EACH):
        out[0, i, 0] = re[i * nu : (i + 1) * nu].astype(out.dtype)
        out[0, i, 1] = im[i * nu : (i + 1) * nu].astype(out.dtype)


def on_device(e_field, h_field, material, eps_table, src_pos, src_amp, freqs):
    rows, cols = material.shape[1:]
    gx, gy = lax.axis_size("gx"), lax.axis_size("gy")
    grid_rows, grid_cols = rows * gx, cols * gy
    wide = EACH * (cols // gx)
    nu = NA // gx
    vb = NA // gy
    col_start = lax.axis_index("gy") * cols
    bf16 = jnp.bfloat16
    angle_index = jnp.arange(NA, dtype=jnp.int32)
    x_tab = table(angle_index - NA // 2, 0, grid_rows, zoom_factor * grid_rows, gx)
    y_cells = col_start + jnp.arange(cols, dtype=jnp.int32)
    y_tab = table(y_cells, NA // 4, NA, zoom_factor * grid_cols, 1)
    e_new, h_new, *sd = yee(e_field, h_field, material, eps_table, src_pos, src_amp)
    turn_re, turn_im = jnp.cos(1.5 * freqs), jnp.sin(1.5 * freqs)
    half_re, half_im = jnp.cos(0.5 * freqs), jnp.sin(0.5 * freqs)
    mix = jnp.stack(
        [turn_re * half_re, turn_im * half_re, -turn_im * half_im, turn_re * half_im], 1
    )
    group = 4
    inv_norm = 1.0 / math.sqrt(grid_rows * grid_cols)
    fars = []
    for sent in sd:
        got = lax.all_to_all(sent, "gx", split_axis=0, concat_axis=0, tiled=True)
        g = pl.pallas_call(
            rows_kernel,
            grid=(gx // group,),
            out_shape=jax.ShapeDtypeStruct((gx, NF, 2, nu, wide), bf16),
            in_specs=[
                SM,
                pl.BlockSpec((group, 2, nu, grid_rows), lambda i: (i, 0, 0, 0)),
                pl.BlockSpec((gx, rows, 2 * wide), lambda i: (0, 0, 0)),
            ],
            out_specs=pl.BlockSpec((group, NF, 2, nu, wide), lambda i: (i, 0, 0, 0, 0)),
            compiler_params=pltpu.CompilerParams(vmem_limit_bytes=BIG),
            name="rows",
        )(mix, x_tab, got)
        moved = lax.all_to_all(g, "gx", split_axis=0, concat_axis=0, tiled=True)
        share = pl.pallas_call(
            cols_kernel,
            grid=(gy,),
            out_shape=jax.ShapeDtypeStruct((gy, NF * EACH, 2, nu, vb), bf16),
            in_specs=[
                pl.BlockSpec((gx, NF, 2, nu, wide), lambda j: (0, 0, 0, 0, 0)),
                pl.BlockSpec((1, 2, cols, vb), lambda j: (0, 0, 0, j)),
            ],
            out_specs=pl.BlockSpec((1, NF * EACH, 2, nu, vb), lambda j: (j, 0, 0, 0, 0)),
            scratch_shapes=[pltpu.VMEM((2, NF * EACH * nu, cols), bf16)],
            compiler_params=pltpu.CompilerParams(vmem_limit_bytes=BIG),
            cost_estimate=pl.CostEstimate(
                flops=16 * NF * EACH * nu * cols * NA, bytes_accessed=16 * nu * NA, transcendentals=0
            ),
            name="cols",
        )(moved, y_tab)
        summed = lax.psum_scatter(share, "gy", scatter_dimension=0, tiled=True)
        scaled = summed[0].astype(jnp.float32) * inv_norm
        fars.append(jnp.transpose(scaled, (2, 0, 1, 3)).reshape(nu, NF, EACH, 2, vb))
    far = jnp.concatenate(fars, 2).reshape(nu, NF * 4, 2, vb)
    shape = e_field.shape
    return (e_new.reshape(shape), h_new.reshape(shape), far)


def solution(mesh):
    placed = (
        P(None, None, "gx", "gy"),
        P(None, None, "gx", "gy"),
        P(None, "gx", "gy"),
        P(),
        P(),
        P(),
        P(),
    )
    return jax.shard_map(
        on_device,
        mesh=mesh,
        in_specs=placed,
        out_specs=(P(None, None, "gx", "gy"), P(None, None, "gx", "gy"), P("gx", None, None, "gy")),
        check_vma=False,
    )
```

profile of v0, /device:TPU:0, one launch (start us, length us, event | category | flops | bytes accessed | tf_op | source)
XLA Modules:
  0.0 224.8 jit_solution(9341382943639954215)
XLA Ops:
  7.2 2.0 fusion.20
  10.2 2.0 fusion.21
  17.6 5.6 %collective-permute-start.1 = (f32[21,2,256]{2,1,0:T(2,128)S(1)}, f32[21,2,256]{2,1,0:T(2,128)S(1)}, u32[]{:S(2)}, u32[]{:S(2)}) collective-permute-start(f32[21,2,256]{2,1,0:T(2,128)S(1)} %maximum_bitcast_fusion.1), channel_id=1, source_target_pairs={{0,1},{1,2},{2,3},{4,5},{5,6},{6,7},{8,9},{9,10},{10,11},{12,13},{... | collective-permute-start | bytes 129032 | tf_op jit(solution)/shard_map/ppermute | solution.py:36
  25.9 2.4 %copy.31 = f32[21,2,256]{1,2,0:T(8,128)} copy(f32[21,2,256]{2,1,0:T(2,128)S(1)} %collective-permute-done) | data formatting | bytes 86016 | tf_op jit(solution)/shard_map/ppermute | solution.py:36
  28.2 2.4 %copy.35 = f32[21,2,256]{1,2,0:T(8,128)} copy(f32[21,2,256]{2,1,0:T(2,128)S(1)} %collective-permute-done.1) | data formatting | bytes 86016 | tf_op jit(solution)/shard_map/ppermute | solution.py:36
  30.6 3.4 %pad_maximum_fusion.colh = f32[21,256,128]{2,1,0:T(8,128)S(1)} fusion(f32[21,256,2]{2,1,0:T(8,128)} %bitcast.32, f32[21,256,2]{2,1,0:T(8,128)} %bitcast.31, f32[128]{0:T(128)S(1)} %pad.18.clone), kind=kLoop, calls=%fused_computation | loop fusion | flops 1376256 | bytes 2839040 | tf_op jit(solution)/shard_map/concatenate | solution.py:241
  35.5 3.0 %collective-permute-start.3 = (f32[21,2,640]{2,1,0:T(2,128)S(1)}, f32[21,2,640]{2,1,0:T(2,128)S(1)}, u32[]{:S(2)}, u32[]{:S(2)}) collective-permute-start(f32[21,2,640]{2,1,0:T(2,128)S(1)} %pad_maximum_fusion.4), channel_id=1, source_target_pairs={{0,4},{4,8},{8,12},{12,16},{16,20},{20,24},{24,28},{1,5},{5,9},{9,... | collective-permute-start | bytes 322568 | tf_op jit(solution)/shard_map/ppermute | solution.py:36
  40.5 22.8 %yee.1 = (f32[9,256,512]{2,1,0:T(8,128)}, f32[9,256,512]{2,1,0:T(8,128)}, bf16[8,256,256]{2,1,0:T(8,128)(2,1)}, bf16[8,256,256]{2,1,0:T(8,128)(2,1)}) custom-call(f32[9,256,512]{2,1,0:T(8,128)} %bitcast.35, f32[9,256,512]{2,1,0:T(8,128)} %bitcast.38, s32[3,256,512]{2,1,0:T(8,128)} %m_hbm.1, f32[21,256,128]{2,1,0:T(8,128)} %copy-done, ...), custom_call_target="tpu_custom_call" | custom-call | tf_op jit(solution)/shard_map/yee/pallas_call | solution.py:254
  63.2 7.1 %all-to-all-start = ((bf16[8,256,256]{2,1,0:T(8,128)(2,1)}), bf16[8,256,256]{2,1,0:T(8,128)(2,1)S(1)}, u32[]{:S(2)}, u32[]{:S(2)}) async-start(bf16[8,256,256]{2,1,0:T(8,128)(2,1)} %get-tuple-element.9), calls=%async_computation | async-start | bytes 2097152 | tf_op jit(solution)/shard_map/all_to_all | solution.py:383
  70.7 3.3 %sine_negate_fusion = (f32[1024,128]{1,0:T(8,128)}, f32[1024,128]{1,0:T(8,128)}) fusion(s32[1024]{0:T(1024)S(1)} %iota_add_fusion), kind=kLoop, calls=%fused_computation.11 | loop fusion | flops 1966080 | bytes 1052672 | tf_op jit(solution)/shard_map/neg | solution.py:293
  73.9 2.8 %sine_negate_fusion.1 = (f32[1024,16]{1,0:T(8,128)}, f32[1024,16]{1,0:T(8,128)}) fusion(f32[1024,16]{1,0:T(8,128)S(1)} %copy.40), kind=kLoop, calls=%fused_computation.14 | loop fusion | flops 32768 | bytes 196608 | tf_op jit(solution)/shard_map/neg | solution.py:293
  76.7 9.3 %chirp.2.tab = bf16[8,2,128,2048]{3,2,1,0:T(8,128)(2,1)} custom-call(f32[1024,16]{1,0:T(8,128)} %get-tuple-element.26.a_re, f32[1024,16]{1,0:T(8,128)} %get-tuple-element.25.a_im, f32[1024,128]{1,0:T(8,128)} %get-tuple-element.30.b_re, f32[1024,128]{1,0:T(8,128)} %get-tuple-element.29.b_im), custom_call_target="tpu_custom_call" | custom-call | flops 16777216 | bytes 8388608 | tf_op jit(solution)/shard_map/chirp/pallas_call | solution.py:305
  87.6 6.1 %rows.2 = bf16[8,2,2,128,128]{4,3,2,1,0:T(8,128)(2,1)} custom-call(f32[2,4]{1,0:T(2,128)} %pad_maximum_fusion.5.mix, bf16[8,2,128,2048]{3,2,1,0:T(8,128)(2,1)} %chirp.2.tab, bf16[8,256,256]{2,1,0:T(8,128)(2,1)} %copy-done.1), custom_call_target="tpu_custom_call" | custom-call | tf_op jit(solution)/shard_map/rows/pallas_call | solution.py:384
  93.6 4.2 %all-to-all-start.1 = ((bf16[8,2,2,128,128]{4,3,2,1,0:T(8,128)(2,1)}), bf16[8,2,2,128,128]{4,3,2,1,0:T(8,128)(2,1)S(1)}, u32[]{:S(2)}, u32[]{:S(2)}) async-start(bf16[8,2,2,128,128]{4,3,2,1,0:T(8,128)(2,1)} %rows.2), calls=%async_computation.1 | async-start | bytes 2097152 | tf_op jit(solution)/shard_map/all_to_all | solution.py:397
  98.1 1.9 sine_negate_fusion.2
  101.7 3.8 %chirp.3.tab = bf16[1,2,512,1024]{3,2,1,0:T(8,128)(2,1)} custom-call(f32[512,8]{1,0:T(8,128)} %get-tuple-element.28.a_re, f32[512,8]{1,0:T(8,128)} %get-tuple-element.27.a_im, f32[512,128]{1,0:T(8,128)} %get-tuple-element.32.b_re, f32[512,128]{1,0:T(8,128)} %get-tuple-element.31.b_im), custom_call_target="tpu_custom_call" | custom-call | flops 4194304 | bytes 2097152 | tf_op jit(solution)/shard_map/chirp/pallas_call | solution.py:305
  105.5 7.7 %all-to-all-done.1.g = bf16[8,2,2,128,128]{4,3,2,1,0:T(8,128)(2,1)S(1)} async-done(((bf16[8,2,2,128,128]{4,3,2,1,0:T(8,128)(2,1)}), bf16[8,2,2,128,128]{4,3,2,1,0:T(8,128)(2,1)S(1)}, u32[]{:S(2)}, u32[]{:S(2)}) %all-to-all-start.1) | async-done | bytes 1048608 | tf_op jit(solution)/shard_map/all_to_all | solution.py:397
  114.2 6.0 %cols.2 = bf16[4,4,2,128,256]{4,3,2,1,0:T(8,128)(2,1)} custom-call(bf16[8,2,2,128,128]{4,3,2,1,0:T(8,128)(2,1)} %copy-done.3, bf16[1,2,512,1024]{3,2,1,0:T(8,128)(2,1)} %chirp.3.tab), custom_call_target="tpu_custom_call" | custom-call | flops 4294967296 | bytes 2097152 | tf_op jit(solution)/shard_map/cols/pallas_call | solution.py:398
  121.5 18.4 %all_to_all.20.v = bf16[8,256,256]{2,1,0:T(8,128)(2,1)} all-to-all(bf16[8,256,256]{2,1,0:T(8,128)(2,1)S(1)} %copy-done.2), channel_id=1, replica_groups=mesh['gx'=8,'gy'=4] {'gx'}, dimensions={0} | all-to-all | bytes 2097152 | tf_op jit(solution)/shard_map/all_to_all | solution.py:383
  139.9 6.1 %rows.3 = bf16[8,2,2,128,128]{4,3,2,1,0:T(8,128)(2,1)} custom-call(f32[2,4]{1,0:T(2,128)} %pad_maximum_fusion.5.mix, bf16[8,2,128,2048]{3,2,1,0:T(8,128)(2,1)} %chirp.2.tab, bf16[8,256,256]{2,1,0:T(8,128)(2,1)} %all_to_all.20.v), custom_call_target="tpu_custom_call" | custom-call | tf_op jit(solution)/shard_map/rows/pallas_call | solution.py:384
  146.0 19.6 %all_to_all.21.g = bf16[8,2,2,128,128]{4,3,2,1,0:T(8,128)(2,1)} all-to-all(bf16[8,2,2,128,128]{4,3,2,1,0:T(8,128)(2,1)} %rows.3), channel_id=1, replica_groups=mesh['gx'=8,'gy'=4] {'gx'}, dimensions={0} | all-to-all | bytes 2097152 | tf_op jit(solution)/shard_map/all_to_all | solution.py:397
  165.5 6.0 %cols.3 = bf16[4,4,2,128,256]{4,3,2,1,0:T(8,128)(2,1)} custom-call(bf16[8,2,2,128,128]{4,3,2,1,0:T(8,128)(2,1)} %all_to_all.21.g, bf16[1,2,512,1024]{3,2,1,0:T(8,128)(2,1)} %chirp.3.tab), custom_call_target="tpu_custom_call" | custom-call | flops 4294967296 | bytes 2097152 | tf_op jit(solution)/shard_map/cols/pallas_call | solution.py:398
  172.8 40.9 %reduce-scatter.5.cloned.1.call-done = bf16[1,4,2,128,256]{4,3,2,1,0:T(8,128)(2,1)} async-done(((bf16[4,4,2,128,256]{4,3,2,1,0:T(8,128)(2,1)}), bf16[1,4,2,128,256]{4,3,2,1,0:T(8,128)(2,1)}) %reduce-scatter.5.cloned.1.call-update) | async-done | bytes 524304 | tf_op jit(solution)/shard_map/reduce_scatter | solution.py:414
  215.0 2.9 %copy.42 = f32[128,2,4,2,256]{4,3,2,1,0:T(2,128)} copy(f32[128,2,4,2,256]{4,0,3,2,1:T(8,128)S(1)} %pad_maximum_fusion.1) | data formatting | bytes 4194304 | tf_op jit(solution)/shard_map/concatenate | solution.py:417
  (61 shorter events, 20.9 us)
Async XLA Ops:
  13.2 12.1 %copy-start.4 = (f32[2]{0:T(128)S(1)}, f32[2]{0:T(128)}, u32[]{:S(2)}) copy-start(f32[2]{0:T(128)} %param.13) | copy-start | bytes 28
  15.4 10.5 %collective-permute-start = (f32[21,2,256]{2,1,0:T(2,128)S(1)}, f32[21,2,256]{2,1,0:T(2,128)S(1)}, u32[]{:S(2)}, u32[]{:S(2)}) collective-permute-start(f32[21,2,256]{2,1,0:T(2,128)S(1)} %maximum_bitcast_fusion), channel_id=1, source_target_pairs={{1,0},{2,1},{3,2},{5,4},{6,5},{7,6},{9,8},{10,9},{11,10},{13,12},{... | collective-permute-start | bytes 129032 | tf_op jit(solution)/shard_map/ppermute | solution.py:36
  17.6 10.6 %collective-permute-start.1 = (f32[21,2,256]{2,1,0:T(2,128)S(1)}, f32[21,2,256]{2,1,0:T(2,128)S(1)}, u32[]{:S(2)}, u32[]{:S(2)}) collective-permute-start(f32[21,2,256]{2,1,0:T(2,128)S(1)} %maximum_bitcast_fusion.1), channel_id=1, source_target_pairs={{0,1},{1,2},{2,3},{4,5},{5,6},{6,7},{8,9},{9,10},{10,11},{12,13},{... | collective-permute-start | bytes 129032 | tf_op jit(solution)/shard_map/ppermute | solution.py:36
  34.0 6.5 %copy-start = (f32[21,256,128]{2,1,0:T(8,128)}, f32[21,256,128]{2,1,0:T(8,128)S(1)}, u32[]{:S(2)}) copy-start(f32[21,256,128]{2,1,0:T(8,128)S(1)} %pad_maximum_fusion.colh) | copy-start | bytes 8257540
  34.1 4.4 %collective-permute-start.2 = (f32[21,2,640]{2,1,0:T(2,128)S(1)}, f32[21,2,640]{2,1,0:T(2,128)S(1)}, u32[]{:S(2)}, u32[]{:S(2)}) collective-permute-start(f32[21,2,640]{2,1,0:T(2,128)S(1)} %pad_maximum_fusion.3), channel_id=1, source_target_pairs={{4,0},{8,4},{12,8},{16,12},{20,16},{24,20},{28,24},{5,1},{9,5},{13... | collective-permute-start | bytes 322568 | tf_op jit(solution)/shard_map/ppermute | solution.py:36
  35.5 4.0 %collective-permute-start.3 = (f32[21,2,640]{2,1,0:T(2,128)S(1)}, f32[21,2,640]{2,1,0:T(2,128)S(1)}, u32[]{:S(2)}, u32[]{:S(2)}) collective-permute-start(f32[21,2,640]{2,1,0:T(2,128)S(1)} %pad_maximum_fusion.4), channel_id=1, source_target_pairs={{0,4},{4,8},{8,12},{12,16},{16,20},{20,24},{24,28},{1,5},{5,9},{9,... | collective-permute-start | bytes 322568 | tf_op jit(solution)/shard_map/ppermute | solution.py:36
  63.2 23.4 %all-to-all-start = ((bf16[8,256,256]{2,1,0:T(8,128)(2,1)}), bf16[8,256,256]{2,1,0:T(8,128)(2,1)S(1)}, u32[]{:S(2)}, u32[]{:S(2)}) async-start(bf16[8,256,256]{2,1,0:T(8,128)(2,1)} %get-tuple-element.9), calls=%async_computation | async-start | bytes 2097152 | tf_op jit(solution)/shard_map/all_to_all | solution.py:383
  86.6 1.0 copy-start.1
  93.6 19.6 %all-to-all-start.1 = ((bf16[8,2,2,128,128]{4,3,2,1,0:T(8,128)(2,1)}), bf16[8,2,2,128,128]{4,3,2,1,0:T(8,128)(2,1)S(1)}, u32[]{:S(2)}, u32[]{:S(2)}) async-start(bf16[8,2,2,128,128]{4,3,2,1,0:T(8,128)(2,1)} %rows.2), calls=%async_computation.1 | async-start | bytes 2097152 | tf_op jit(solution)/shard_map/all_to_all | solution.py:397
  97.8 73.8 %reduce-scatter.3.cloned.1.call-start = ((), (), s32[]{:S(2)}) async-start(), calls=%async_computation.6 | async-start | bytes 2621440 | tf_op jit(solution)/shard_map/reduce_scatter | solution.py:414
  113.2 1.0 copy-start.3
  120.2 1.2 copy-start.2
  120.3 93.4 %reduce-scatter.5.cloned.1.call-start = ((), (), s32[]{:S(2)}) async-start(), calls=%async_computation.7 | async-start | bytes 2621440 | tf_op jit(solution)/shard_map/reduce_scatter | solution.py:414
Sparse Core Ops, SparseCore 0:
  120.4 41.9 reduce-scatter.2
  171.7 41.9 reduce-scatter.4
where the time goes:
time: 226 us; the launch traced here: 225 us
  Pallas kernels  60 us (27%)
  waiting for transfers between devices  49.6 us (22%)
  blocking collectives  38 us (17%)
  starting transfers between devices  22.6 us (10%)
  local copies, waits for them, and re-layouts  21.2 us (9%)
  other arithmetic  19.1 us (8%)
  between operations  14.3 us (6%)
    reduce_scatter x2, waiting for transfers between devices, on_device(): summed = lax.psum_scatter(share, 'gy', scatter_dimension=0, tiled=True)  41 us
    pallas_call x1, Pallas kernels, yee(): pl.pallas_call(functools.partial(yee_kernel, grid_rows, grid_cols, gx), o...  22.8 us
    all_to_all x1, blocking collectives, on_device(): moved = lax.all_to_all(g, 'gx', split_axis=0, concat_axis=0, tiled=True)  19.6 us
    all_to_all x1, blocking collectives, on_device(): got = lax.all_to_all(sent, 'gx', split_axis=0, concat_axis=0, tiled=True)  18.4 us
    pallas_call x2, Pallas kernels, table(): pl.pallas_call(table_kernel, grid=(blocks,), out_shape=jax.ShapeDtypeStru...  13.1 us
    pallas_call x2, Pallas kernels, on_device(): pl.pallas_call(rows_kernel, grid=(gx // group,), out_shape=jax.ShapeDtype...  12.1 us
    pallas_call x2, Pallas kernels, on_device(): pl.pallas_call(cols_kernel, grid=(gy,), out_shape=jax.ShapeDtypeStruct((g...  12.1 us
    ppermute x4, starting transfers between devices, shifted(): return lax.ppermute(block, axis, route)  11.2 us
  transfers between devices with their start and end apart: 8, of which 3 were waited for; matrix products, arithmetic and copies ran while one was open for 8% of the time, Pallas kernels for 11%

commit v1 on v0

--- a/solution.py
+++ b/solution.py
@@ -23,6 +23,7 @@
 CHUNK = 16
 SETS = 2
 EACH = 4 // SETS
+LANES = 128
 PAD = 128
 ANY = pl.BlockSpec(memory_space=pl.ANY)
 VM = pl.BlockSpec(memory_space=pltpu.VMEM)
@@ -36,8 +37,12 @@
     return lax.ppermute(block, axis, route)
 
 
+def fields_per_device(gx, cols):
+    return 2 * EACH * cols // (gx * LANES)
+
+
 def yee_kernel(
-    grid_rows, grid_cols, gx,
+    grid_rows, grid_cols, per,
     e_hbm, h_hbm, m_hbm, colh, rowh, eps, pos, amp,
     e_out, h_out, *rest,
 ):
@@ -192,13 +197,12 @@
                     if last:
                         old = first[item, now, :]
                         here = pl.ds(r - BASE, CHUNK)
-                        span = cols // gx
-                        place = (item % EACH) * span
                         for which, value in enumerate((old + face, face - old)):
-                            lo = which * EACH * span + place
-                            for j in range(gx):
-                                piece = value[:, j * span : (j + 1) * span].astype(jnp.bfloat16)
-                                sd_outs[item // EACH][j, here, lo : lo + span] = piece
+                            share, place = divmod(which * EACH + item % EACH, per)
+                            for q in range(cols // LANES):
+                                piece = value[:, q * LANES : (q + 1) * LANES].astype(jnp.bfloat16)
+                                lanes = pl.ds(place * LANES, LANES)
+                                sd_outs[item // EACH][q * (2 * EACH // per) + share, here, lanes] = piece
                     else:
                         first[item, now, :] = face
         return carry
@@ -221,6 +225,7 @@
 def yee(e_field, h_field, material, eps_table, src_pos, src_amp):
     rows, cols = material.shape[1:]
     gx = lax.axis_size("gx")
+    per = fields_per_device(gx, cols)
     grid_rows = rows * gx
     grid_cols = cols * lax.axis_size("gy")
     planes = 3 * LZ
@@ -252,12 +257,12 @@
     width = cols + PAD
     f32 = jnp.float32
     out = pl.pallas_call(
-        functools.partial(yee_kernel, grid_rows, grid_cols, gx),
+        functools.partial(yee_kernel, grid_rows, grid_cols, per),
         out_shape=(
             jax.ShapeDtypeStruct((planes, rows, cols), f32),
             jax.ShapeDtypeStruct((planes, rows, cols), f32),
         )
-        + (jax.ShapeDtypeStruct((gx, rows, 2 * EACH * (cols // gx)), jnp.bfloat16),) * SETS,
+        + (jax.ShapeDtypeStruct((gx, rows, per * LANES), jnp.bfloat16),) * SETS,
         in_specs=[ANY, ANY, ANY, VM, VM, SM, VM, VM],
         out_specs=(ANY, ANY) + (VM,) * SETS,
         scratch_shapes=[
@@ -278,145 +283,280 @@
     return out
 
 
-def table_kernel(a_re, a_im, b_re, b_im, out):
-    lo_re, lo_im = b_re[...], b_im[...]
-    for block in range(a_re.shape[1]):
-        hi_re = a_re[:, block : block + 1]
-        hi_im = a_im[:, block : block + 1]
-        at = slice(block * 128, block * 128 + 128)
-        out[0, 0, :, at] = (hi_re * lo_re - hi_im * lo_im).astype(jnp.bfloat16)
-        out[0, 1, :, at] = (hi_re * lo_im + hi_im * lo_re).astype(jnp.bfloat16)
+SIN = (-1.0 / 6.0, 1.0 / 120.0, -1.0 / 5040.0, 1.0 / 362880.0)
+COS = (-0.5, 1.0 / 24.0, -1.0 / 720.0, 1.0 / 40320.0, -1.0 / 3628800.0)
 
 
 def unit(phase, period):
-    angle = jnp.remainder(phase, period).astype(jnp.float32) * (2.0 * math.pi / period)
-    return jnp.cos(angle), -jnp.sin(angle)
-
-
-def table(row_index, first, length, period, blocks):
-    count = row_index.shape[0]
-    high = first + 128 * jnp.arange(length // 128, dtype=jnp.int32)
-    low = jnp.arange(128, dtype=jnp.int32)
-    a_re, a_im = unit(row_index[:, None] * high[None, :], period)
-    b_re, b_im = unit(row_index[:, None] * low[None, :], period)
-    size = count // blocks
-    one = pl.BlockSpec((size, length // 128), lambda i: (i, 0))
-    two = pl.BlockSpec((size, 128), lambda i: (i, 0))
-    return pl.pallas_call(
-        table_kernel,
-        grid=(blocks,),
-        out_shape=jax.ShapeDtypeStruct((blocks, 2, size, length), jnp.bfloat16),
-        in_specs=[one, one, two, two],
-        out_specs=pl.BlockSpec((1, 2, size, length), lambda i: (i, 0, 0, 0)),
-        cost_estimate=pl.CostEstimate(
-            flops=8 * count * length, bytes_accessed=4 * count * length, transcendentals=0
-        ),
-        name="chirp",
-    )(a_re, a_im, b_re, b_im)
-
-
-def rows_kernel(mix, tab, v, out):
-    group, _, nu, depth = tab.shape
-    half = v.shape[2] // 2
-    left = tab[...].reshape(group * 2 * nu, depth)
-    right = v[...].reshape(depth, 2 * half)
-    both = jnp.dot(left, right, preferred_element_type=jnp.float32)
-    both = both.reshape(group, 2, nu, 2 * half)
-    for b in range(group):
-        s_re, s_im = both[b, 0, :, :half], both[b, 1, :, :half]
-        d_re, d_im = both[b, 0, :, half:], both[b, 1, :, half:]
-        for f in range(NF):
-            p_re, p_im, q_re, q_im = (mix[f, i] for i in range(4))
-            re = p_re * s_re - p_im * s_im + (q_re * d_re - q_im * d_im)
-            im = p_re * s_im + p_im * s_re + (q_re * d_im + q_im * d_re)
-            out[b, f, 0] = re.astype(jnp.bfloat16)
-            out[b, f, 1] = im.astype(jnp.bfloat16)
-
-
-def cols_kernel(g, tab, out, left):
-    gx, _, _, nu, wide = g.shape
-    span = wide // EACH
-
-    @pl.when(pl.program_id(0) == 0)
-    def _():
-        for f in range(NF):
-            for c in range(2):
-                got = [g[j, f, c].astype(jnp.float32) for j in range(gx)]
-                for k in range(EACH):
-                    at = (f * EACH + k) * nu
-                    row = [piece[:, k * span : (k + 1) * span] for piece in got]
-                    left[c, at : at + nu, :] = jnp.concatenate(row, 1).astype(jnp.bfloat16)
-
-    y_re = tab[0, 0]
-    y_im = tab[0, 1]
+    eighth = period // 8
+    turn = phase & (period - 1)
+    quarter = (turn + eighth) // (2 * eighth)
+    x = (turn - quarter * (2 * eighth)).astype(jnp.float32) * (2.0 * math.pi / period)
+    square = x * x
+    sine = jnp.full_like(x, SIN[-1])
+    for factor in SIN[-2::-1]:
+        sine = sine * square + factor
+    sine = x + x * (square * sine)
+    cosine = jnp.full_like(x, COS[-1])
+    for factor in COS[-2::-1]:
+        cosine = cosine * square + factor
+    cosine = 1.0 + square * cosine
+    odd = (quarter & 1) == 1
+    re = jnp.where(odd, sine, cosine)
+    im = jnp.where(odd, cosine, sine)
+    re = jnp.where(((quarter + 1) & 2) == 2, -re, re)
+    im = jnp.where((quarter & 2) == 2, im, -im)
+    return re, im
+
+
+def far_kernel(grid_rows, grid_cols, mix, *rest):
+    sd, out, rest = rest[:SETS], rest[SETS], rest[SETS + 1 :]
+    x_tab, y_tab, v, g, left, held, got, *sems = rest
+    send_v, recv_v, send_g, recv_g, send_f, recv_f = sems
+    gx, gy = lax.axis_size("gx"), lax.axis_size("gy")
+    i, z = lax.axis_index("gx"), lax.axis_index("gy")
+    me = i * gy + z
+    count = gx * gy
+    rows = grid_rows // gx
+    cols = grid_cols // gy
+    per = v.shape[2] // LANES
+    split = 2 * EACH // per
+    slabs = cols // LANES
+    own = x_tab.shape[1]
+    nper = own // 2
+    vb = NA // gy
+    mesh_id = pl.DeviceIdType.MESH
+
+    barrier = pltpu.get_barrier_semaphore()
+    for offset in range(1, count):
+        peer = lax.rem(me + offset, count)
+        pl.semaphore_signal(
+            barrier, inc=1, device_id=(lax.div(peer, gy), lax.rem(peer, gy)), device_id_type=mesh_id
+        )
+    pl.semaphore_wait(barrier, count - 1)
+
+    def v_copy(s, offset):
+        peer = lax.rem(i + offset, gx)
+        here = pl.ds(pl.multiple_of(i * rows, rows), rows)
+        return pltpu.make_async_remote_copy(
+            src_ref=sd[s].at[peer],
+            dst_ref=v.at[s, here],
+            send_sem=send_v.at[s, offset],
+            recv_sem=recv_v.at[s, offset],
+            device_id=(peer, z),
+            device_id_type=mesh_id,
+        )
+
+    def v_own(s):
+        here = pl.ds(pl.multiple_of(i * rows, rows), rows)
+        return pltpu.make_async_copy(sd[s].at[i], v.at[s, here], recv_v.at[s, 0])
+
+    def g_place(s):
+        share = lax.rem(i, split) * per
+        lane = (z * slabs + lax.div(i, split)) * LANES
+        return left.at[s, pl.ds(share, per), :, pl.ds(pl.multiple_of(lane, LANES), LANES)]
+
+    def g_part(s, peer):
+        return g.at[s, :, pl.ds(pl.multiple_of(peer * own, own), own), :]
+
+    def g_copy(s, peer):
+        offset = lax.rem(peer - me + count, count)
+        return pltpu.make_async_remote_copy(
+            src_ref=g_part(s, peer),
+            dst_ref=g_place(s),
+            send_sem=send_g.at[s, offset],
+            recv_sem=recv_g.at[s, offset],
+            device_id=(lax.div(peer, gy), lax.rem(peer, gy)),
+            device_id_type=mesh_id,
+        )
+
+    def g_own(s):
+        return pltpu.make_async_copy(g_part(s, me), g_place(s), recv_g.at[s, 0])
+
+    def f_copy(s, offset):
+        peer = lax.rem(z + offset, gy)
+        return pltpu.make_async_remote_copy(
+            src_ref=held.at[s, peer],
+            dst_ref=got.at[s, z],
+            send_sem=send_f.at[s, offset],
+            recv_sem=recv_f.at[s, offset],
+            device_id=(i, peer),
+            device_id_type=mesh_id,
+        )
+
+    def build_x():
+        low = lax.broadcasted_iota(jnp.int32, (nper, LANES), 1)
+        row = lax.broadcasted_iota(jnp.int32, (nper, LANES), 0) - NA // 2
+
+        def body(d, carry):
+            u = row + d * nper
+            a_re, a_im = unit(u * (low * LANES), zoom_factor * grid_rows)
+            b_re, b_im = unit(u * low, zoom_factor * grid_rows)
+            for block in range(grid_rows // LANES):
+                h_re, h_im = a_re[:, block : block + 1], a_im[:, block : block + 1]
+                re = h_re * b_re - h_im * b_im
+                im = h_re * b_im + h_im * b_re
+                both = jnp.concatenate([re, im], 0).astype(jnp.bfloat16)
+                x_tab[d, :, block * LANES : (block + 1) * LANES] = both
+            return carry
+
+        lax.fori_loop(0, count, body, 0)
+
+    def build_y():
+        tall = 32
+        low = lax.broadcasted_iota(jnp.int32, (tall, LANES), 1)
+        row = lax.broadcasted_iota(jnp.int32, (tall, LANES), 0)
+
+        def body(d, carry):
+            start = pl.multiple_of(d * tall, tall)
+            y = row + start
+            a_re, a_im = unit(y * (low * LANES + NA // 4), zoom_factor * grid_cols)
+            b_re, b_im = unit(y * low, zoom_factor * grid_cols)
+            for block in range(NA // LANES):
+                h_re, h_im = a_re[:, block : block + 1], a_im[:, block : block + 1]
+                at = slice(block * LANES, (block + 1) * LANES)
+                y_tab[0, pl.ds(start, tall), at] = (h_re * b_re - h_im * b_im).astype(jnp.bfloat16)
+                y_tab[1, pl.ds(start, tall), at] = (h_re * b_im + h_im * b_re).astype(jnp.bfloat16)
+            return carry
+
+        lax.fori_loop(0, grid_cols // tall, body, 0)
+
     dot = functools.partial(jnp.dot, preferred_element_type=jnp.float32)
-    re = dot(left[0], y_re) - dot(left[1], y_im)
-    im = dot(left[0], y_im) + dot(left[1], y_re)
-    for i in range(NF * EACH):
-        out[0, i, 0] = re[i * nu : (i + 1) * nu].astype(out.dtype)
-        out[0, i, 1] = im[i * nu : (i + 1) * nu].astype(out.dtype)
-
-
-def on_device(e_field, h_field, material, eps_table, src_pos, src_amp, freqs):
-    rows, cols = material.shape[1:]
+    group = 2 * gy
+    parts = count // group
+
+    def transform_rows(s):
+        v_own(s).wait()
+        for offset in range(1, gx):
+            v_copy(s, offset).wait_recv()
+
+        def body(c, carry):
+            chunk = lax.rem(lax.div(me, group) + 1 + c, parts)
+            block = x_tab[pl.ds(chunk * group, group)].reshape(group * own, grid_rows)
+            both = dot(block, v[s]).astype(jnp.bfloat16)
+            here = pl.ds(pl.multiple_of(chunk * (group * own), group * own), group * own)
+            for f in range(per):
+                g[s, f, here, :] = both[:, f * LANES : (f + 1) * LANES]
+            for e in range(group):
+                peer = chunk * group + e
+
+                @pl.when(peer != me)
+                def _():
+                    g_copy(s, peer).start()
+
+                @pl.when(peer == me)
+                def _():
+                    g_own(s).start()
+
+            return carry
+
+        lax.fori_loop(0, parts, body, 0)
+
+    def transform_cols(s):
+        g_own(s).wait()
+        for offset in range(1, count):
+            g_copy(s, lax.rem(me + offset, count)).wait_recv()
+        lhs = left[s].reshape(2 * EACH * own, grid_cols)
+        for step in range(1, gy + 1):
+            peer = lax.rem(z + step, gy)
+            at = pl.ds(pl.multiple_of(peer * vb, vb), vb)
+            p_re = dot(lhs, y_tab[0, :, at])
+            p_im = dot(lhs, y_tab[1, :, at])
+            for f in range(2 * EACH):
+                top = slice(f * own, f * own + nper)
+                low = slice(f * own + nper, (f + 1) * own)
+                re = (p_re[top] - p_im[low]).astype(jnp.bfloat16)
+                im = (p_im[top] + p_re[low]).astype(jnp.bfloat16)
+                if step < gy:
+                    held[s, peer, f, 0] = re
+                    held[s, peer, f, 1] = im
+                else:
+                    got[s, z, f, 0] = re
+                    got[s, z, f, 1] = im
+            if step < gy:
+                f_copy(s, step).start()
+
+    for s in range(SETS):
+        v_own(s).start()
+        for offset in range(1, gx):
+            v_copy(s, offset).start()
+    build_x()
+    transform_rows(0)
+    build_y()
+    for s in range(1, SETS):
+        transform_rows(s)
+    for s in range(SETS):
+        transform_cols(s)
+    for s in range(SETS):
+        for offset in range(1, gy):
+            f_copy(s, offset).wait_recv()
+        for src in range(gy):
+            at = slice(src * nper, (src + 1) * nper)
+            for k in range(EACH):
+                s_re = got[s, src, k, 0].astype(jnp.float32)
+                s_im = got[s, src, k, 1].astype(jnp.float32)
+                d_re = got[s, src, EACH + k, 0].astype(jnp.float32)
+                d_im = got[s, src, EACH + k, 1].astype(jnp.float32)
+                for f in range(NF):
+                    p_re, p_im, q_re, q_im = (mix[f, t] for t in range(4))
+                    item = f * 4 + s * EACH + k
+                    out[item, 0, at, :] = p_re * s_re - p_im * s_im + (q_re * d_re - q_im * d_im)
+                    out[item, 1, at, :] = p_re * s_im + p_im * s_re + (q_re * d_im + q_im * d_re)
+    for s in range(SETS):
+        for offset in range(1, gx):
+            v_copy(s, offset).wait_send()
+        for offset in range(1, count):
+            g_copy(s, lax.rem(me + offset, count)).wait_send()
+        for offset in range(1, gy):
+            f_copy(s, offset).wait_send()
+
+
+def far(sd, freqs, grid_rows, grid_cols):
     gx, gy = lax.axis_size("gx"), lax.axis_size("gy")
-    grid_rows, grid_cols = rows * gx, cols * gy
-    wide = EACH * (cols // gx)
-    nu = NA // gx
-    vb = NA // gy
-    col_start = lax.axis_index("gy") * cols
+    count = gx * gy
+    nu, vb, nper = NA // gx, NA // gy, NA // count
+    wide = sd[0].shape[2]
     bf16 = jnp.bfloat16
-    angle_index = jnp.arange(NA, dtype=jnp.int32)
-    x_tab = table(angle_index - NA // 2, 0, grid_rows, zoom_factor * grid_rows, gx)
-    y_cells = col_start + jnp.arange(cols, dtype=jnp.int32)
-    y_tab = table(y_cells, NA // 4, NA, zoom_factor * grid_cols, 1)
-    e_new, h_new, *sd = yee(e_field, h_field, material, eps_table, src_pos, src_amp)
     turn_re, turn_im = jnp.cos(1.5 * freqs), jnp.sin(1.5 * freqs)
     half_re, half_im = jnp.cos(0.5 * freqs), jnp.sin(0.5 * freqs)
     mix = jnp.stack(
         [turn_re * half_re, turn_im * half_re, -turn_im * half_im, turn_re * half_im], 1
-    )
-    group = 4
-    inv_norm = 1.0 / math.sqrt(grid_rows * grid_cols)
-    fars = []
-    for sent in sd:
-        got = lax.all_to_all(sent, "gx", split_axis=0, concat_axis=0, tiled=True)
-        g = pl.pallas_call(
-            rows_kernel,
-            grid=(gx // group,),
-            out_shape=jax.ShapeDtypeStruct((gx, NF, 2, nu, wide), bf16),
-            in_specs=[
-                SM,
-                pl.BlockSpec((group, 2, nu, grid_rows), lambda i: (i, 0, 0, 0)),
-                pl.BlockSpec((gx, rows, 2 * wide), lambda i: (0, 0, 0)),
-            ],
-            out_specs=pl.BlockSpec((group, NF, 2, nu, wide), lambda i: (i, 0, 0, 0, 0)),
-            compiler_params=pltpu.CompilerParams(vmem_limit_bytes=BIG),
-            name="rows",
-        )(mix, x_tab, got)
-        moved = lax.all_to_all(g, "gx", split_axis=0, concat_axis=0, tiled=True)
-        share = pl.pallas_call(
-            cols_kernel,
-            grid=(gy,),
-            out_shape=jax.ShapeDtypeStruct((gy, NF * EACH, 2, nu, vb), bf16),
-            in_specs=[
-                pl.BlockSpec((gx, NF, 2, nu, wide), lambda j: (0, 0, 0, 0, 0)),
-                pl.BlockSpec((1, 2, cols, vb), lambda j: (0, 0, 0, j)),
-            ],
-            out_specs=pl.BlockSpec((1, NF * EACH, 2, nu, vb), lambda j: (j, 0, 0, 0, 0)),
-            scratch_shapes=[pltpu.VMEM((2, NF * EACH * nu, cols), bf16)],
-            compiler_params=pltpu.CompilerParams(vmem_limit_bytes=BIG),
-            cost_estimate=pl.CostEstimate(
-                flops=16 * NF * EACH * nu * cols * NA, bytes_accessed=16 * nu * NA, transcendentals=0
-            ),
-            name="cols",
-        )(moved, y_tab)
-        summed = lax.psum_scatter(share, "gy", scatter_dimension=0, tiled=True)
-        scaled = summed[0].astype(jnp.float32) * inv_norm
-        fars.append(jnp.transpose(scaled, (2, 0, 1, 3)).reshape(nu, NF, EACH, 2, vb))
-    far = jnp.concatenate(fars, 2).reshape(nu, NF * 4, 2, vb)
+    ) * (1.0 / math.sqrt(grid_rows * grid_cols))
+    dma = pltpu.SemaphoreType.DMA
+    done = pl.pallas_call(
+        functools.partial(far_kernel, grid_rows, grid_cols),
+        out_shape=jax.ShapeDtypeStruct((NF * 4, 2, nu, vb), jnp.float32),
+        in_specs=[SM] + [ANY] * SETS,
+        out_specs=VM,
+        scratch_shapes=[
+            pltpu.VMEM((count, 2 * nper, grid_rows), bf16),
+            pltpu.VMEM((2, grid_cols, NA), bf16),
+            pltpu.VMEM((SETS, grid_rows, wide), bf16),
+            pltpu.VMEM((SETS, wide // LANES, 2 * NA, LANES), bf16),
+            pltpu.VMEM((SETS, 2 * EACH, 2 * nper, grid_cols), bf16),
+            pltpu.VMEM((SETS, gy, 2 * EACH, 2, nper, vb), bf16),
+            pltpu.VMEM((SETS, gy, 2 * EACH, 2, nper, vb), bf16),
+            dma((SETS, gx)),
+            dma((SETS, gx)),
+            dma((SETS, count)),
+            dma((SETS, count)),
+            dma((SETS, gy)),
+            dma((SETS, gy)),
+        ],
+        compiler_params=pltpu.CompilerParams(
+            vmem_limit_bytes=BIG, collective_id=1, has_side_effects=True
+        ),
+        name="far",
+    )(mix, *sd)
+    return jnp.transpose(done, (2, 0, 1, 3))
+
+
+def on_device(e_field, h_field, material, eps_table, src_pos, src_amp, freqs):
+    rows, cols = material.shape[1:]
+    grid_rows, grid_cols = rows * lax.axis_size("gx"), cols * lax.axis_size("gy")
+    e_new, h_new, *sd = yee(e_field, h_field, material, eps_table, src_pos, src_amp)
     shape = e_field.shape
-    return (e_new.reshape(shape), h_new.reshape(shape), far)
+    return (e_new.reshape(shape), h_new.reshape(shape), far(sd, freqs, grid_rows, grid_cols))
 
 
 def solution(mesh):

time: 226 us -> 153 us (0.68)
  Pallas kernels: 60 us -> 113 us
  waiting for transfers between devices: 49.6 us -> 0.29 us
  blocking collectives: 38 us -> 0 us
  between operations: 14.3 us -> 0.77 us
  other arithmetic: 19.1 us -> 6.9 us
  starting transfers between devices: 22.6 us -> 11.2 us
    pallas_call x7 -> x2, Pallas kernels: 60 us -> 113 us  [the longest x1 90.6 us: far(): pl.pallas_call(functools.partial(far_kernel, grid_rows, grid_cols), out_s...]
    reduce_scatter x2 -> x0, waiting for transfers between devices: 41 us -> none  [on_device(): summed = lax.psum_scatter(share, 'gy', scatter_dimension=0, tiled=True)]
    all_to_all x2 -> x0, blocking collectives: 38 us -> none  [the longest x1 19.6 us: on_device(): moved = lax.all_to_all(g, 'gx', split_axis=0, concat_axis=0, tiled=True)]
    all_to_all x2 -> x0, starting transfers between devices: 11.3 us -> none  [the longest x1 7.13 us: on_device(): got = lax.all_to_all(sent, 'gx', split_axis=0, concat_axis=0, tiled=True)]
    neg x4 -> x0, other arithmetic: 9.65 us -> none  [unit(): return (jnp.cos(angle), -jnp.sin(angle))]
    all_to_all x2 -> x0, waiting for transfers between devices: 7.69 us -> none  [the longest x1 7.69 us: on_device(): moved = lax.all_to_all(g, 'gx', split_axis=0, concat_axis=0, tiled=True)]
    concatenate x1 -> x0, local copies, waits for them, and re-layouts: 2.94 us -> none  [on_device(): far = jnp.concatenate(fars, 2).reshape(nu, NF * 4, 2, vb)]
    unnamed x12 -> x7, local copies, waits for them, and re-layouts: 3.44 us -> 4.84 us
  transfers between devices with their start and end apart: 8 -> 4, of which waited for: 3 -> 1; matrix products, arithmetic and copies ran while one was open for 8% -> 4% of each run, Pallas kernels for 11% -> 0%
where the time goes in v1:
time: 153 us; the launch traced here: 151 us
  Pallas kernels  113 us (74%)
  local copies, waits for them, and re-layouts  19.3 us (13%)
  starting transfers between devices  11.2 us (7%)
  other arithmetic  6.9 us (5%)
    pallas_call x1, Pallas kernels, far(): pl.pallas_call(functools.partial(far_kernel, grid_rows, grid_cols), out_s...  90.6 us
    pallas_call x1, Pallas kernels, yee(): pl.pallas_call(functools.partial(yee_kernel, grid_rows, grid_cols, per),...  21.9 us
    ppermute x4, starting transfers between devices, shifted(): return lax.ppermute(block, axis, route)  11.2 us
    slice x8, local copies, waits for them, and re-layouts, edge(): cut = lambda a: lax.slice_in_dim(a, low, high, axis=dim)  9.21 us
    unnamed x7, local copies, waits for them, and re-layouts  4.84 us
    ppermute x2, local copies, waits for them, and re-layouts, shifted(): return lax.ppermute(block, axis, route)  4.74 us
    concatenate x1, other arithmetic, yee(): jnp.concatenate([right, jnp.zeros((total, rows, PAD - 4), jnp.float32), l...  3.38 us
  transfers between devices with their start and end apart: 4, of which 1 were waited for; matrix products, arithmetic and copies ran while one was open for 4% of the time, Pallas kernels for 0%

profile of v1, /device:TPU:0, one launch (start us, length us, event | category | flops | bytes accessed | tf_op | source)
XLA Modules:
  0.0 151.0 jit_solution(12839515839689090856)
XLA Ops:
  0.6 2.0 %fusion.2 = (f32[9,256,2]{2,1,0:T(8,128)S(1)}, f32[9,256,2]{2,1,0:T(8,128)S(1)}) fusion(f32[9,256,512]{2,1,0:T(8,128)} %bitcast.23), kind=kLoop, calls=%fused_computation.19 | loop fusion | bytes 73728 | tf_op jit(solution)/shard_map/slice | solution.py:236
  2.7 1.0 copy.16
  3.6 2.0 %fusion.3 = (f32[9,256,2]{2,1,0:T(8,128)S(1)}, f32[9,256,2]{2,1,0:T(8,128)S(1)}) fusion(f32[9,256,512]{2,1,0:T(8,128)} %bitcast.26), kind=kLoop, calls=%fused_computation.20 | loop fusion | bytes 73728 | tf_op jit(solution)/shard_map/slice | solution.py:236
  5.7 1.0 copy.17
  6.6 1.3 fusion.5
  8.1 0.8 maximum_bitcast_fusion
  8.9 1.3 collective-permute-start
  10.2 0.4 copy.20
  10.5 0.4 copy.21
  10.9 0.2 copy.29
  11.1 5.6 %collective-permute-start.1 = (f32[21,2,256]{2,1,0:T(2,128)S(1)}, f32[21,2,256]{2,1,0:T(2,128)S(1)}, u32[]{:S(2)}, u32[]{:S(2)}) collective-permute-start(f32[21,2,256]{2,1,0:T(2,128)S(1)} %maximum_bitcast_fusion.1), channel_id=1, source_target_pairs={{0,1},{1,2},{2,3},{4,5},{5,6},{6,7},{8,9},{9,10},{10,11},{12,13},{... | collective-permute-start | bytes 129032 | tf_op jit(solution)/shard_map/ppermute | solution.py:37
  16.7 1.2 fusion
  17.9 0.8 slice_convert_fusion.1
  19.3 2.4 %copy.18 = f32[21,2,256]{1,2,0:T(8,128)} copy(f32[21,2,256]{2,1,0:T(2,128)S(1)} %collective-permute-done) | data formatting | bytes 86016 | tf_op jit(solution)/shard_map/ppermute | solution.py:37
  21.7 2.4 %copy.22 = f32[21,2,256]{1,2,0:T(8,128)} copy(f32[21,2,256]{2,1,0:T(2,128)S(1)} %collective-permute-done.1) | data formatting | bytes 86016 | tf_op jit(solution)/shard_map/ppermute | solution.py:37
  24.1 3.4 %pad_maximum_fusion.colh = f32[21,256,128]{2,1,0:T(8,128)S(1)} fusion(f32[21,256,2]{2,1,0:T(8,128)} %bitcast.22, f32[21,256,2]{2,1,0:T(8,128)} %bitcast.21, f32[128]{0:T(128)S(1)} %pad.16.clone), kind=kLoop, calls=%fused_computation | loop fusion | flops 1376256 | bytes 2839040 | tf_op jit(solution)/shard_map/concatenate | solution.py:246
  27.6 1.3 collective-permute-start.2
  28.9 3.0 %collective-permute-start.3 = (f32[21,2,640]{2,1,0:T(2,128)S(1)}, f32[21,2,640]{2,1,0:T(2,128)S(1)}, u32[]{:S(2)}, u32[]{:S(2)}) collective-permute-start(f32[21,2,640]{2,1,0:T(2,128)S(1)} %pad_maximum_fusion.3), channel_id=1, source_target_pairs={{0,4},{4,8},{8,12},{12,16},{16,20},{20,24},{24,28},{1,5},{5,9},{9,... | collective-permute-start | bytes 322568 | tf_op jit(solution)/shard_map/ppermute | solution.py:37
  32.0 0.7 maximum_multiply_fusion.mix
  32.6 0.3 collective-permute-done.3
  32.9 1.1 pad_maximum_fusion.1.rowh
  34.0 21.9 %yee.1 = (f32[9,256,512]{2,1,0:T(8,128)}, f32[9,256,512]{2,1,0:T(8,128)}, bf16[8,256,256]{2,1,0:T(8,128)(2,1)}, bf16[8,256,256]{2,1,0:T(8,128)(2,1)}) custom-call(f32[9,256,512]{2,1,0:T(8,128)} %bitcast.25, f32[9,256,512]{2,1,0:T(8,128)} %bitcast.28, s32[3,256,512]{2,1,0:T(8,128)} %m_hbm.1, f32[21,256,128]{2,1,0:T(8,128)} %copy-done, ...), custom_call_target="tpu_custom_call" | custom-call | tf_op jit(solution)/shard_map/yee/pallas_call | solution.py:259
  55.9 90.6 %far.1 = f32[8,2,128,256]{3,2,1,0:T(8,128)} custom-call(f32[2,4]{1,0:T(2,128)} %maximum_multiply_fusion.mix, bf16[8,256,256]{2,1,0:T(8,128)(2,1)} %get-tuple-element.9.rest_0_, bf16[8,256,256]{2,1,0:T(8,128)(2,1)} %get-tuple-element.10.rest_1_), custom_call_target="tpu_custom_call" | custom-call | tf_op jit(solution)/shard_map/far/pallas_call | solution.py:526
  146.5 4.5 %copy.27 = f32[128,8,2,256]{3,2,1,0:T(2,128)} copy(f32[128,8,2,256]{3,0,2,1:T(8,128)} %bitcast.29) | data formatting | bytes 4194304
  (23 shorter events, 0.9 us)
Async XLA Ops:
  6.6 12.1 %copy-start.1 = (f32[2]{0:T(128)S(1)}, f32[2]{0:T(128)}, u32[]{:S(2)}) copy-start(f32[2]{0:T(128)} %param.13) | copy-start | bytes 28
  8.9 10.5 %collective-permute-start = (f32[21,2,256]{2,1,0:T(2,128)S(1)}, f32[21,2,256]{2,1,0:T(2,128)S(1)}, u32[]{:S(2)}, u32[]{:S(2)}) collective-permute-start(f32[21,2,256]{2,1,0:T(2,128)S(1)} %maximum_bitcast_fusion), channel_id=1, source_target_pairs={{1,0},{2,1},{3,2},{5,4},{6,5},{7,6},{9,8},{10,9},{11,10},{13,12},{... | collective-permute-start | bytes 129032 | tf_op jit(solution)/shard_map/ppermute | solution.py:37
  11.1 10.6 %collective-permute-start.1 = (f32[21,2,256]{2,1,0:T(2,128)S(1)}, f32[21,2,256]{2,1,0:T(2,128)S(1)}, u32[]{:S(2)}, u32[]{:S(2)}) collective-permute-start(f32[21,2,256]{2,1,0:T(2,128)S(1)} %maximum_bitcast_fusion.1), channel_id=1, source_target_pairs={{0,1},{1,2},{2,3},{4,5},{5,6},{6,7},{8,9},{9,10},{10,11},{12,13},{... | collective-permute-start | bytes 129032 | tf_op jit(solution)/shard_map/ppermute | solution.py:37
  27.5 6.5 %copy-start = (f32[21,256,128]{2,1,0:T(8,128)}, f32[21,256,128]{2,1,0:T(8,128)S(1)}, u32[]{:S(2)}) copy-start(f32[21,256,128]{2,1,0:T(8,128)S(1)} %pad_maximum_fusion.colh) | copy-start | bytes 8257540
  27.6 5.1 %collective-permute-start.2 = (f32[21,2,640]{2,1,0:T(2,128)S(1)}, f32[21,2,640]{2,1,0:T(2,128)S(1)}, u32[]{:S(2)}, u32[]{:S(2)}) collective-permute-start(f32[21,2,640]{2,1,0:T(2,128)S(1)} %pad_maximum_fusion.2), channel_id=1, source_target_pairs={{4,0},{8,4},{12,8},{16,12},{20,16},{24,20},{28,24},{5,1},{9,5},{13... | collective-permute-start | bytes 322568 | tf_op jit(solution)/shard_map/ppermute | solution.py:37
  28.9 4.0 %collective-permute-start.3 = (f32[21,2,640]{2,1,0:T(2,128)S(1)}, f32[21,2,640]{2,1,0:T(2,128)S(1)}, u32[]{:S(2)}, u32[]{:S(2)}) collective-permute-start(f32[21,2,640]{2,1,0:T(2,128)S(1)} %pad_maximum_fusion.3), channel_id=1, source_target_pairs={{0,4},{4,8},{8,12},{12,16},{16,20},{20,24},{24,28},{1,5},{5,9},{9,... | collective-permute-start | bytes 322568 | tf_op jit(solution)/shard_map/ppermute | solution.py:37

commit v2 on v1

--- a/solution.py
+++ b/solution.py
@@ -31,10 +31,150 @@
 BIG = 60 * 1024 * 1024
 
 
-def shifted(block, axis, distance):
-    size = lax.axis_size(axis)
-    route = [(i - distance, i) for i in range(size) if 0 <= i - distance < size]
-    return lax.ppermute(block, axis, route)
+def halo_kernel(
+    e, h, m, col_rim, corner, rim_f, rim_m,
+    edge_f, edge_m, packed, got_col, got_corner, got_f, got_m, load, send, recv,
+):
+    gx, gy = lax.axis_size("gx"), lax.axis_size("gy")
+    i, z = lax.axis_index("gx"), lax.axis_index("gy")
+    planes, rows, cols = e.shape
+    around = [(a, b) for a in (-1, 0, 1) for b in (-1, 0, 1) if (a, b) != (0, 0)]
+
+    def exists(step):
+        row, col = i + step[0], z + step[1]
+        return (row >= 0) & (row < gx) & (col >= 0) & (col < gy)
+
+    loads = []
+    for side, lane in enumerate((0, cols - LANES)):
+        at = pl.ds(lane, LANES)
+        loads.append(pltpu.make_async_copy(e.at[:, :, at], edge_f.at[side, pl.ds(0, planes)], load.at[3 * side]))
+        loads.append(pltpu.make_async_copy(h.at[:, :, at], edge_f.at[side, pl.ds(planes, planes)], load.at[3 * side + 1]))
+        loads.append(pltpu.make_async_copy(m.at[:, :, at], edge_m.at[side], load.at[3 * side + 2]))
+    for copy in loads:
+        copy.start()
+    barrier = pltpu.get_barrier_semaphore()
+    total = jnp.int32(0)
+    for step in around:
+        total += exists(step).astype(jnp.int32)
+
+        @pl.when(exists(step))
+        def _():
+            pl.semaphore_signal(
+                barrier, inc=1, device_id=(i + step[0], z + step[1]), device_id_type=pl.DeviceIdType.MESH
+            )
+
+    pl.semaphore_wait(barrier, total)
+
+    def remote(step, src, dst, index):
+        copy = pltpu.make_async_remote_copy(
+            src_ref=src, dst_ref=dst, send_sem=send.at[index], recv_sem=recv.at[index],
+            device_id=(i + step[0], z + step[1]), device_id_type=pl.DeviceIdType.MESH,
+        )
+        return step, copy
+
+    rows_out, cols_out = [], []
+    for side, low in enumerate((0, rows - 8)):
+        step = (2 * side - 1, 0)
+        at = pl.ds(low, 8)
+        rows_out.append(remote(step, e.at[:, at, :], got_f.at[side, pl.ds(0, planes)], 3 * side))
+        rows_out.append(remote(step, h.at[:, at, :], got_f.at[side, pl.ds(planes, planes)], 3 * side + 1))
+        rows_out.append(remote(step, m.at[:, at, :], got_m.at[side], 3 * side + 2))
+    for side in range(2):
+        cols_out.append(remote((0, 2 * side - 1), packed.at[side], got_col.at[side], 6 + side))
+        for end, low in enumerate((0, rows - 8)):
+            step = (2 * end - 1, 2 * side - 1)
+            src = packed.at[side, pl.ds(low, 8)]
+            cols_out.append(remote(step, src, got_corner.at[end, side], 8 + 2 * side + end))
+
+    def start(copies):
+        for step, copy in copies:
+
+            @pl.when(exists(step))
+            def _():
+                copy.start()
+
+    start(rows_out)
+    for copy in loads:
+        copy.wait()
+    tall = 32
+    lane = lax.broadcasted_iota(jnp.int32, (tall, LANES), 1)
+
+    def pack(c, carry):
+        at = pl.ds(pl.multiple_of(c * tall, tall), tall)
+        for side in range(2):
+            place = ((lane + 2 * side) & (LANES - 1)) >> 2
+            block = jnp.zeros((tall, LANES), jnp.float32)
+            for p in range(2 * planes + LZ):
+                if p < 2 * planes:
+                    piece = edge_f[side, p, at, :]
+                else:
+                    piece = edge_m[side, p - 2 * planes, at, :].astype(jnp.float32)
+                block = jnp.where(place == p, pltpu.roll(piece, 4 * p, 1), block)
+            packed[side, at, :] = block
+        return carry
+
+    lax.fori_loop(0, rows // tall, pack, 0)
+    start(cols_out)
+    for step, copy in rows_out + cols_out:
+
+        @pl.when(exists((-step[0], -step[1])))
+        def _():
+            copy.wait_recv()
+
+    last = (lane & 2) == 0
+    after, before = exists((0, 1)), exists((0, -1))
+
+    def merge(c, carry):
+        at = pl.ds(pl.multiple_of(c * tall, tall), tall)
+        right = jnp.where(after, got_col[0, at, :], 0.0)
+        left = jnp.where(before, got_col[1, at, :], 0.0)
+        col_rim[at, :] = jnp.where(last, right, left)
+        return carry
+
+    lax.fori_loop(0, rows // tall, merge, 0)
+    for side in range(2):
+        there = exists((1 - 2 * side, 0))
+        rim_f[side] = jnp.where(there, got_f[side], 0.0)
+        rim_m[side] = jnp.where(there, got_m[side], 0)
+        right = jnp.where(there & after, got_corner[side, 0], 0.0)
+        left = jnp.where(there & before, got_corner[side, 1], 0.0)
+        corner[side] = jnp.where(last[:8], right, left)
+    for step, copy in rows_out + cols_out:
+
+        @pl.when(exists(step))
+        def _():
+            copy.wait_send()
+
+
+def halo(e, h, m):
+    planes, rows, cols = e.shape
+    f32, i32 = jnp.float32, jnp.int32
+    dma = pltpu.SemaphoreType.DMA
+    return pl.pallas_call(
+        halo_kernel,
+        out_shape=(
+            jax.ShapeDtypeStruct((rows, LANES), f32),
+            jax.ShapeDtypeStruct((2, 8, LANES), f32),
+            jax.ShapeDtypeStruct((2, 2 * planes, 8, cols), f32),
+            jax.ShapeDtypeStruct((2, LZ, 8, cols), i32),
+        ),
+        in_specs=[ANY] * 3,
+        out_specs=(VM,) * 4,
+        scratch_shapes=[
+            pltpu.VMEM((2, 2 * planes, rows, LANES), f32),
+            pltpu.VMEM((2, LZ, rows, LANES), i32),
+            pltpu.VMEM((2, rows, LANES), f32),
+            pltpu.VMEM((2, rows, LANES), f32),
+            pltpu.VMEM((2, 2, 8, LANES), f32),
+            pltpu.VMEM((2, 2 * planes, 8, cols), f32),
+            pltpu.VMEM((2, LZ, 8, cols), i32),
+            dma((6,)),
+            dma((12,)),
+            dma((12,)),
+        ],
+        compiler_params=pltpu.CompilerParams(collective_id=0, has_side_effects=True),
+        name="halo",
+    )(e, h, m)
 
 
 def fields_per_device(gx, cols):
@@ -43,7 +183,7 @@
 
 def yee_kernel(
     grid_rows, grid_cols, per,
-    e_hbm, h_hbm, m_hbm, colh, rowh, eps, pos, amp,
+    e_hbm, h_hbm, m_hbm, col_rim, corner, rim_f, rim_m, eps, pos, amp,
     e_out, h_out, *rest,
 ):
     sd_outs, (e_ext, h_ext, m_main, scale, src, first, sems) = rest[:SETS], rest[SETS:]
@@ -101,37 +241,46 @@
     col_pad = col0 + jnp.where(lane_pad < PAD // 2, cols + lane_pad, lane_pad - PAD)
     row_chunk = row0 + lax.broadcasted_iota(jnp.int32, (CHUNK, cols), 0)
 
+    def shown(block, plane):
+        return pltpu.roll(block, PAD - 4 * plane, 1) if plane else block
+
     def fill(step_index, carry):
         r = pl.multiple_of(step_index * CHUNK, CHUNK)
         near = pl.ds(r, CHUNK)
         far = pl.ds(BASE + r, CHUNK)
+        block = col_rim[near, :]
         for layer in range(LZ):
             scale[layer, far, :cols] = scale_of(m_main[layer, near, :], row_chunk + r, col_main)
             scale[layer, far, cols:] = scale_of(
-                colh[6 * LZ + layer, near, :], row_chunk[:, :PAD] + r, col_pad
+                shown(block, 6 * LZ + layer), row_chunk[:, :PAD] + r, col_pad
             )
         for plane in range(3 * LZ):
-            e_ext[plane, far, cols:] = colh[plane, near, :]
-            h_ext[plane, far, cols:] = colh[3 * LZ + plane, near, :]
+            e_ext[plane, far, cols:] = shown(block, plane)
+            h_ext[plane, far, cols:] = shown(block, 3 * LZ + plane)
         return carry
 
     lax.fori_loop(0, rows // CHUNK, fill, 0)
-    lane_all = lax.broadcasted_iota(jnp.int32, (8, width), 1)
-    col_all = col0 + jnp.where(lane_all < cols + PAD // 2, lane_all, lane_all - width)
-    row_eight = row0 + lax.broadcasted_iota(jnp.int32, (8, width), 0)
+    row_eight = row0 + lax.broadcasted_iota(jnp.int32, (8, cols), 0)
     blank = jnp.zeros((8, width), jnp.float32)
-    for place, target, offset, spare in (
+    for side, target, offset, spare in (
         (0, BASE + rows, rows, BASE + rows + 8),
-        (8, BASE - 8, -8, BASE - 16),
+        (1, BASE - 8, -8, BASE - 16),
     ):
+        here = slice(target, target + 8)
+        block = corner[side]
         for layer in range(LZ):
-            scale[layer, target : target + 8, :] = scale_of(
-                rowh[6 * LZ + layer, place : place + 8, :], row_eight + offset, col_all
+            scale[layer, here, :cols] = scale_of(
+                rim_m[side, layer], row_eight + offset, col_main[:8]
+            )
+            scale[layer, here, cols:] = scale_of(
+                shown(block, 6 * LZ + layer), row_eight[:, :PAD] + offset, col_pad[:8]
             )
             scale[layer, spare : spare + 8, :] = blank
         for plane in range(3 * LZ):
-            e_ext[plane, target : target + 8, :] = rowh[plane, place : place + 8, :]
-            h_ext[plane, target : target + 8, :] = rowh[3 * LZ + plane, place : place + 8, :]
+            e_ext[plane, here, :cols] = rim_f[side, plane]
+            h_ext[plane, here, :cols] = rim_f[side, 3 * LZ + plane]
+            e_ext[plane, here, cols:] = shown(block, plane)
+            h_ext[plane, here, cols:] = shown(block, 3 * LZ + plane)
             e_ext[plane, spare : spare + 8, :] = blank
             h_ext[plane, spare : spare + 8, :] = blank
     for plane in range(3 * LZ):
@@ -232,27 +381,6 @@
     e = e_field.reshape(planes, rows, cols)
     h = h_field.reshape(planes, rows, cols)
 
-    def edge(low, high, dim):
-        cut = lambda a: lax.slice_in_dim(a, low, high, axis=dim)
-        return jnp.concatenate([cut(e), cut(h), cut(material).astype(jnp.float32)], 0)
-
-    send_prev = jnp.swapaxes(edge(0, 2, 2), 1, 2)
-    send_next = jnp.swapaxes(edge(cols - 2, cols, 2), 1, 2)
-    right = shifted(send_prev, "gy", -1)
-    left = shifted(send_next, "gy", 1)
-    right = jnp.swapaxes(right, 1, 2)
-    left = jnp.swapaxes(left, 1, 2)
-    total = 2 * planes + LZ
-    col_halo = jnp.concatenate(
-        [right, jnp.zeros((total, rows, PAD - 4), jnp.float32), left], 2
-    )
-    send_up = jnp.concatenate([edge(0, 2, 1), col_halo[:, 0:2]], 2)
-    send_down = jnp.concatenate([edge(rows - 2, rows, 1), col_halo[:, rows - 2 :]], 2)
-    below = shifted(send_up, "gx", -1)
-    above = shifted(send_down, "gx", 1)
-    row_halo = jnp.concatenate(
-        [below, jnp.zeros((total, 12, cols + PAD), jnp.float32), above], 1
-    )
     high = rows + 2 * BASE
     width = cols + PAD
     f32 = jnp.float32
@@ -263,7 +391,7 @@
             jax.ShapeDtypeStruct((planes, rows, cols), f32),
         )
         + (jax.ShapeDtypeStruct((gx, rows, per * LANES), jnp.bfloat16),) * SETS,
-        in_specs=[ANY, ANY, ANY, VM, VM, SM, VM, VM],
+        in_specs=[ANY, ANY, ANY, VM, VM, VM, VM, SM, VM, VM],
         out_specs=(ANY, ANY) + (VM,) * SETS,
         scratch_shapes=[
             pltpu.VMEM((planes, high, width), f32),
@@ -277,7 +405,7 @@
         compiler_params=pltpu.CompilerParams(vmem_limit_bytes=BIG),
         name="yee",
     )(
-        e, h, material, col_halo, row_halo,
+        e, h, material, *halo(e, h, material),
         eps_table, jnp.swapaxes(src_pos, 0, 1), src_amp[None, :],
     )
     return out

time: 153 us -> 131 us (0.86)
  local copies, waits for them, and re-layouts: 19.3 us -> 4.9 us
  starting transfers between devices: 11.2 us -> 0 us
  Pallas kernels: 113 us -> 123 us
  other arithmetic: 6.9 us -> 1.3 us
    pallas_call x0 -> x1, Pallas kernels: none -> 12.6 us  [halo(): pl.pallas_call(halo_kernel, out_shape=(jax.ShapeDtypeStruct((rows, LANES)...]
    ppermute x4 -> x0, starting transfers between devices: 11.2 us -> none  [shifted(): return lax.ppermute(block, axis, route)]
    slice x9 -> x0, local copies, waits for them, and re-layouts: 9.23 us -> none  [the longest x8 9.21 us: edge(): cut = lambda a: lax.slice_in_dim(a, low, high, axis=dim)]
    ppermute x2 -> x0, local copies, waits for them, and re-layouts: 4.74 us -> none  [shifted(): return lax.ppermute(block, axis, route)]
    concatenate x4 -> x0, other arithmetic: 4.54 us -> none  [the longest x1 3.38 us: yee(): jnp.concatenate([right, jnp.zeros((total, rows, PAD - 4), jnp.float32), l...]
    pallas_call x1, Pallas kernels: 90.6 us -> 88.8 us  [far(): pl.pallas_call(functools.partial(far_kernel, grid_rows, grid_cols), out_s...]
    unnamed x7 -> x1, local copies, waits for them, and re-layouts: 4.84 us -> 4.53 us
  transfers between devices with their start and end apart: 4 -> 0, of which waited for: 1 -> 0; matrix products, arithmetic and copies ran while one was open for 4% -> 0% of each run, Pallas kernels for 0% -> 0%
where the time goes in v2:
time: 131 us; the launch traced here: 130 us
  Pallas kernels  123 us (94%)
  local copies, waits for them, and re-layouts  4.9 us (4%)
    pallas_call x1, Pallas kernels, far(): pl.pallas_call(functools.partial(far_kernel, grid_rows, grid_cols), out_s...  88.8 us
    pallas_call x1, Pallas kernels, yee(): pl.pallas_call(functools.partial(yee_kernel, grid_rows, grid_cols, per),...  21.3 us
    pallas_call x1, Pallas kernels, halo(): pl.pallas_call(halo_kernel, out_shape=(jax.ShapeDtypeStruct((rows, LANES)...  12.6 us
    unnamed x1, local copies, waits for them, and re-layouts  4.53 us

profile of v2, /device:TPU:0, one launch (start us, length us, event | category | flops | bytes accessed | tf_op | source)
XLA Modules:
  0.0 129.5 jit_solution(11149953872452100310)
XLA Ops:
  0.6 0.7 multiply_bitcast_fusion.3
  1.3 0.1 copy.10
  1.4 0.1 copy.11
  1.5 0.1 copy.13
  1.6 0.1 copy.12
  1.7 0.6 maximum_multiply_fusion.mix
  2.3 12.6 %halo.1 = (f32[256,128]{1,0:T(8,128)}, f32[2,8,128]{2,1,0:T(8,128)}, f32[2,18,8,512]{3,2,1,0:T(8,128)}, s32[2,3,8,512]{3,2,1,0:T(8,128)}) custom-call(f32[9,256,512]{2,1,0:T(8,128)} %bitcast.15, f32[9,256,512]{2,1,0:T(8,128)} %bitcast.17, s32[3,256,512]{2,1,0:T(8,128)} %m_hbm.1), custom_call_target="tpu_custom_call" | custom-call | tf_op jit(solution)/shard_map/halo/pallas_call | solution.py:153
  14.9 21.3 %yee.1 = (f32[9,256,512]{2,1,0:T(8,128)}, f32[9,256,512]{2,1,0:T(8,128)}, bf16[8,256,256]{2,1,0:T(8,128)(2,1)}, bf16[8,256,256]{2,1,0:T(8,128)(2,1)}) custom-call(f32[9,256,512]{2,1,0:T(8,128)} %bitcast.16, f32[9,256,512]{2,1,0:T(8,128)} %bitcast.18, s32[3,256,512]{2,1,0:T(8,128)} %m_hbm.1, f32[256,128]{1,0:T(8,128)} %get-tuple-element.11.col_rim, ...), custom_call_target="tpu_custom_call" | custom-call | tf_op jit(solution)/shard_map/yee/pallas_call | solution.py:387
  36.2 88.8 %far.1 = f32[8,2,128,256]{3,2,1,0:T(8,128)} custom-call(f32[2,4]{1,0:T(2,128)} %maximum_multiply_fusion.mix, bf16[8,256,256]{2,1,0:T(8,128)(2,1)} %get-tuple-element.17.rest_0_, bf16[8,256,256]{2,1,0:T(8,128)(2,1)} %get-tuple-element.18.rest_1_), custom_call_target="tpu_custom_call" | custom-call | tf_op jit(solution)/shard_map/far/pallas_call | solution.py:654
  125.0 4.5 %copy.14 = f32[128,8,2,256]{3,2,1,0:T(2,128)} copy(f32[128,8,2,256]{3,0,2,1:T(8,128)} %bitcast.19) | data formatting | bytes 4194304

commit v3 on v2

--- a/solution.py
+++ b/solution.py
@@ -437,10 +437,15 @@
     return re, im
 
 
+def layout(gx, gy):
+    mper = max(8, NA // 2 // (gx * gy))
+    return mper, NA // 2 // mper, NA // gx // mper
+
+
 def far_kernel(grid_rows, grid_cols, mix, *rest):
-    sd, out, rest = rest[:SETS], rest[SETS], rest[SETS + 1 :]
-    x_tab, y_tab, v, g, left, held, got, *sems = rest
-    send_v, recv_v, send_g, recv_g, send_f, recv_f = sems
+    sd, outs, rest = rest[:SETS], rest[SETS : 2 * SETS], rest[2 * SETS :]
+    x_tab, y_tab, v, g, left, left_x, held, held_x, *sems = rest
+    send_v, recv_v, send_g, recv_g, send_x, recv_x, send_f, recv_f, send_1, recv_1, send_e = sems
     gx, gy = lax.axis_size("gx"), lax.axis_size("gy")
     i, z = lax.axis_index("gx"), lax.axis_index("gy")
     me = i * gy + z
@@ -450,10 +455,46 @@
     per = v.shape[2] // LANES
     split = 2 * EACH // per
     slabs = cols // LANES
-    own = x_tab.shape[1]
-    nper = own // 2
+    mper, owners, near = layout(gx, gy)
+    own = 2 * mper
     vb = NA // gy
+    wide = NF * EACH * 2
+    half = gx // 2
     mesh_id = pl.DeviceIdType.MESH
+
+    upper = i >= half
+    plane = jnp.where(upper, i - half, half - 1 - i)
+    turn = jnp.where(upper, 0, gy) + z
+    block_id = plane * near + turn
+
+    def owner(t):
+        c, r = lax.div(t, near), lax.rem(t, near)
+        return jnp.where(r < gy, half + c, half - 1 - c), lax.rem(r, gy)
+
+    end_i, end_z = owner(jnp.int32(owners - 1))
+
+    def ship(src, dst, where, send_sem, recv_sem, start):
+        here = (where[0] == i) & (where[1] == z)
+
+        @pl.when(~here)
+        def _():
+            copy = pltpu.make_async_remote_copy(
+                src_ref=src, dst_ref=dst, send_sem=send_sem, recv_sem=recv_sem,
+                device_id=where, device_id_type=mesh_id,
+            )
+            if start:
+                copy.start()
+            else:
+                copy.wait_send()
+
+        if start:
+
+            @pl.when(here)
+            def _():
+                pltpu.make_async_copy(src, dst, recv_sem).start()
+
+    def arrived(ref, sem):
+        pltpu.make_async_copy(ref, ref, sem).wait()
 
     barrier = pltpu.get_barrier_semaphore()
     for offset in range(1, count):
@@ -463,72 +504,74 @@
         )
     pl.semaphore_wait(barrier, count - 1)
 
-    def v_copy(s, offset):
+    def v_ship(s, offset, start):
         peer = lax.rem(i + offset, gx)
         here = pl.ds(pl.multiple_of(i * rows, rows), rows)
-        return pltpu.make_async_remote_copy(
-            src_ref=sd[s].at[peer],
-            dst_ref=v.at[s, here],
-            send_sem=send_v.at[s, offset],
-            recv_sem=recv_v.at[s, offset],
-            device_id=(peer, z),
-            device_id_type=mesh_id,
+        ship(sd[s].at[peer], v.at[s, here], (peer, z), send_v.at[s, offset], recv_v.at[s, i], start)
+
+    def g_ship(s, t, start):
+        lane = pl.multiple_of((z * slabs + lax.div(i, split)) * LANES, LANES)
+        to = (pl.ds(lax.rem(i, split) * per, per), slice(None), pl.ds(lane, LANES))
+        part = g.at[s, :, pl.ds(pl.multiple_of(t * own, own), own), :]
+        ship(part, left.at[(s, *to)], owner(t), send_g.at[s, t], recv_g.at[s, me], start)
+
+    def x_ship(s, start):
+        lane = pl.multiple_of((z * slabs + lax.div(i, split)) * LANES, LANES)
+        to = (pl.ds(lax.rem(i, split) * per, per), slice(None), pl.ds(lane, LANES))
+        part = g.at[s, :, pl.ds(owners * own, 16), :]
+        ship(part, left_x.at[(s, *to)], (end_i, end_z), send_x.at[s], recv_x.at[s, me], start)
+
+    def f_ship(s, step, start):
+        peer = lax.rem(z + step, gy)
+        at = pl.ds(pl.multiple_of(turn * mper, mper), mper)
+        ship(
+            held.at[s, peer, 0], outs[s].at[at], (half + plane, peer),
+            send_f.at[s, 0, step - 1], recv_f.at[s, turn], start,
         )
-
-    def v_own(s):
-        here = pl.ds(pl.multiple_of(i * rows, rows), rows)
-        return pltpu.make_async_copy(sd[s].at[i], v.at[s, here], recv_v.at[s, 0])
-
-    def g_place(s):
-        share = lax.rem(i, split) * per
-        lane = (z * slabs + lax.div(i, split)) * LANES
-        return left.at[s, pl.ds(share, per), :, pl.ds(pl.multiple_of(lane, LANES), LANES)]
-
-    def g_part(s, peer):
-        return g.at[s, :, pl.ds(pl.multiple_of(peer * own, own), own), :]
-
-    def g_copy(s, peer):
-        offset = lax.rem(peer - me + count, count)
-        return pltpu.make_async_remote_copy(
-            src_ref=g_part(s, peer),
-            dst_ref=g_place(s),
-            send_sem=send_g.at[s, offset],
-            recv_sem=recv_g.at[s, offset],
-            device_id=(lax.div(peer, gy), lax.rem(peer, gy)),
-            device_id_type=mesh_id,
+        mirror = near - 1 - turn
+        at = pl.ds(mirror * mper + 1, mper - 1)
+        ship(
+            held.at[s, peer, 1, pl.ds(0, mper - 1)], outs[s].at[at], (half - 1 - plane, peer),
+            send_f.at[s, 1, step - 1], recv_f.at[s, mirror], start,
         )
-
-    def g_own(s):
-        return pltpu.make_async_copy(g_part(s, me), g_place(s), recv_g.at[s, 0])
-
-    def f_copy(s, offset):
-        peer = lax.rem(z + offset, gy)
-        return pltpu.make_async_remote_copy(
-            src_ref=held.at[s, peer],
-            dst_ref=got.at[s, z],
-            send_sem=send_f.at[s, offset],
-            recv_sem=recv_f.at[s, offset],
-            device_id=(i, peer),
-            device_id_type=mesh_id,
+        first = turn == 0
+        to = jnp.where(first, half - plane, half - 1 - plane)
+        slot = jnp.where(first, 0, near - turn)
+
+        @pl.when(block_id > 0)
+        def _():
+            ship(
+                held.at[s, peer, 1, pl.ds(mper - 1, 1)], outs[s].at[pl.ds(slot * mper, 1)], (to, peer),
+                send_1.at[s, step - 1], recv_1.at[s, slot], start,
+            )
+
+    def e_ship(s, step, start):
+        peer = lax.rem(z + step, gy)
+        ship(
+            held_x.at[s, peer], outs[s].at[pl.ds(0, 1)], (0, peer),
+            send_e.at[s, step - 1], recv_1.at[s, 0], start,
         )
 
+    def fill_x(m, row):
+        low = lax.broadcasted_iota(jnp.int32, m.shape, 1)
+        a_re, a_im = unit(m * (low * LANES), zoom_factor * grid_rows)
+        b_re, b_im = unit(m * low, zoom_factor * grid_rows)
+        for block in range(grid_rows // LANES):
+            h_re, h_im = a_re[:, block : block + 1], a_im[:, block : block + 1]
+            re = h_re * b_re - h_im * b_im
+            im = h_re * b_im + h_im * b_re
+            both = jnp.concatenate([re, im], 0).astype(jnp.bfloat16)
+            x_tab[pl.ds(row, 2 * m.shape[0]), block * LANES : (block + 1) * LANES] = both
+
     def build_x():
-        low = lax.broadcasted_iota(jnp.int32, (nper, LANES), 1)
-        row = lax.broadcasted_iota(jnp.int32, (nper, LANES), 0) - NA // 2
-
-        def body(d, carry):
-            u = row + d * nper
-            a_re, a_im = unit(u * (low * LANES), zoom_factor * grid_rows)
-            b_re, b_im = unit(u * low, zoom_factor * grid_rows)
-            for block in range(grid_rows // LANES):
-                h_re, h_im = a_re[:, block : block + 1], a_im[:, block : block + 1]
-                re = h_re * b_re - h_im * b_im
-                im = h_re * b_im + h_im * b_re
-                both = jnp.concatenate([re, im], 0).astype(jnp.bfloat16)
-                x_tab[d, :, block * LANES : (block + 1) * LANES] = both
+        row = lax.broadcasted_iota(jnp.int32, (mper, LANES), 0)
+
+        def body(t, carry):
+            fill_x(row + t * mper, pl.multiple_of(t * own, own))
             return carry
 
-        lax.fori_loop(0, count, body, 0)
+        lax.fori_loop(0, owners, body, 0)
+        fill_x(jnp.full((8, LANES), NA // 2, jnp.int32), owners * own)
 
     def build_y():
         tall = 32
@@ -550,100 +593,151 @@
         lax.fori_loop(0, grid_cols // tall, body, 0)
 
     dot = functools.partial(jnp.dot, preferred_element_type=jnp.float32)
-    group = 2 * gy
-    parts = count // group
+    parts = 2
+    group = owners // parts
 
     def transform_rows(s):
-        v_own(s).wait()
-        for offset in range(1, gx):
-            v_copy(s, offset).wait_recv()
+        for src in range(gx):
+            arrived(v.at[s, pl.ds(src * rows, rows)], recv_v.at[s, src])
 
         def body(c, carry):
-            chunk = lax.rem(lax.div(me, group) + 1 + c, parts)
-            block = x_tab[pl.ds(chunk * group, group)].reshape(group * own, grid_rows)
-            both = dot(block, v[s]).astype(jnp.bfloat16)
-            here = pl.ds(pl.multiple_of(chunk * (group * own), group * own), group * own)
+            chunk = lax.rem(lax.div(block_id, group) + 1 + c, parts)
+            tall = group * own
+            start = pl.multiple_of(chunk * tall, tall)
+            both = dot(x_tab[pl.ds(start, tall + 16), :], v[s]).astype(jnp.bfloat16)
             for f in range(per):
-                g[s, f, here, :] = both[:, f * LANES : (f + 1) * LANES]
+                g[s, f, pl.ds(start, tall), :] = both[:tall, f * LANES : (f + 1) * LANES]
+
+            @pl.when(chunk == parts - 1)
+            def _():
+                for f in range(per):
+                    g[s, f, owners * own :, :] = both[tall:, f * LANES : (f + 1) * LANES]
+                x_ship(s, True)
+
             for e in range(group):
-                peer = chunk * group + e
-
-                @pl.when(peer != me)
-                def _():
-                    g_copy(s, peer).start()
-
-                @pl.when(peer == me)
-                def _():
-                    g_own(s).start()
-
+                g_ship(s, chunk * group + e, True)
             return carry
 
         lax.fori_loop(0, parts, body, 0)
 
+    def one_hot(shape, source):
+        row = lax.broadcasted_iota(jnp.int32, shape, 0)
+        col = lax.broadcasted_iota(jnp.int32, shape, 1)
+        return jnp.where(col == source(row), 1.0, 0.0).astype(jnp.bfloat16)
+
+    size = (wide * mper, wide * mper)
+    forth = one_hot(size, lambda row: lax.rem(row, wide) * mper + lax.div(row, wide))
+    back = one_hot(size, lambda row: lax.rem(row, wide) * mper + mper - 1 - lax.div(row, wide))
+    only = one_hot((wide, wide * 8), lambda row: row * 8)
+
+    def finish(lhs, count_m, peer):
+        at = pl.ds(pl.multiple_of(peer * vb, vb), vb)
+        p_re, p_im = dot(lhs, y_tab[0, :, at]), dot(lhs, y_tab[1, :, at])
+        plus, minus = [], []
+
+        def both_signs(f):
+            top = slice(2 * f * count_m, (2 * f + 1) * count_m)
+            low = slice((2 * f + 1) * count_m, (2 * f + 2) * count_m)
+            a_re, a_im, b_re, b_im = p_re[top], p_im[top], p_re[low], p_im[low]
+            return (a_re - b_im, a_im + b_re), (a_re + b_im, a_im - b_re)
+
+        fields = [both_signs(f) for f in range(2 * EACH)]
+        for f in range(NF):
+            p0, p1, q0, q1 = (mix[f, t] for t in range(4))
+            for k in range(EACH):
+                for sign, result in enumerate((plus, minus)):
+                    s_re, s_im = fields[k][sign]
+                    d_re, d_im = fields[EACH + k][sign]
+                    result.append(p0 * s_re - p1 * s_im + (q0 * d_re - q1 * d_im))
+                    result.append(p0 * s_im + p1 * s_re + (q0 * d_im + q1 * d_re))
+        pack = lambda result: jnp.concatenate(result, 0).astype(jnp.bfloat16)
+        return pack(plus), pack(minus)
+
     def transform_cols(s):
-        g_own(s).wait()
-        for offset in range(1, count):
-            g_copy(s, lax.rem(me + offset, count)).wait_recv()
+        for src in range(count):
+            src_i, src_z = divmod(src, gy)
+            lane = (src_z * slabs + src_i // split) * LANES
+            region = left.at[s, pl.ds(src_i % split * per, per), :, pl.ds(lane, LANES)]
+            arrived(region, recv_g.at[s, src])
         lhs = left[s].reshape(2 * EACH * own, grid_cols)
         for step in range(1, gy + 1):
             peer = lax.rem(z + step, gy)
-            at = pl.ds(pl.multiple_of(peer * vb, vb), vb)
-            p_re = dot(lhs, y_tab[0, :, at])
-            p_im = dot(lhs, y_tab[1, :, at])
-            for f in range(2 * EACH):
-                top = slice(f * own, f * own + nper)
-                low = slice(f * own + nper, (f + 1) * own)
-                re = (p_re[top] - p_im[low]).astype(jnp.bfloat16)
-                im = (p_im[top] + p_re[low]).astype(jnp.bfloat16)
-                if step < gy:
-                    held[s, peer, f, 0] = re
-                    held[s, peer, f, 1] = im
-                else:
-                    got[s, z, f, 0] = re
-                    got[s, z, f, 1] = im
-            if step < gy:
-                f_copy(s, step).start()
+            plus, minus = finish(lhs, mper, peer)
+            held[s, peer, 0] = dot(forth, plus).reshape(mper, wide, vb).astype(jnp.bfloat16)
+            held[s, peer, 1] = dot(back, minus).reshape(mper, wide, vb).astype(jnp.bfloat16)
+            f_ship(s, step, True)
+
+    at_end = (i == end_i) & (z == end_z)
+
+    def transform_end(s):
+        for src in range(count):
+            src_i, src_z = divmod(src, gy)
+            lane = (src_z * slabs + src_i // split) * LANES
+            region = left_x.at[s, pl.ds(src_i % split * per, per), :, pl.ds(lane, LANES)]
+            arrived(region, recv_x.at[s, src])
+        lhs = left_x[s].reshape(2 * EACH * 16, grid_cols)
+        for step in range(1, gy + 1):
+            peer = lax.rem(z + step, gy)
+            _, minus = finish(lhs, 8, peer)
+            held_x[s, peer] = dot(only, minus).reshape(1, wide, vb).astype(jnp.bfloat16)
+            e_ship(s, step, True)
+
+    def owned(body):
+        if near == 2 * gy:
+            body()
+        else:
+            pl.when(turn < near)(body)
 
     for s in range(SETS):
-        v_own(s).start()
-        for offset in range(1, gx):
-            v_copy(s, offset).start()
+        for offset in range(gx):
+            v_ship(s, offset, True)
     build_x()
     transform_rows(0)
     build_y()
     for s in range(1, SETS):
         transform_rows(s)
     for s in range(SETS):
-        transform_cols(s)
+        owned(functools.partial(transform_cols, s))
+        pl.when(at_end)(functools.partial(transform_end, s))
     for s in range(SETS):
-        for offset in range(1, gy):
-            f_copy(s, offset).wait_recv()
-        for src in range(gy):
-            at = slice(src * nper, (src + 1) * nper)
-            for k in range(EACH):
-                s_re = got[s, src, k, 0].astype(jnp.float32)
-                s_im = got[s, src, k, 1].astype(jnp.float32)
-                d_re = got[s, src, EACH + k, 0].astype(jnp.float32)
-                d_im = got[s, src, EACH + k, 1].astype(jnp.float32)
-                for f in range(NF):
-                    p_re, p_im, q_re, q_im = (mix[f, t] for t in range(4))
-                    item = f * 4 + s * EACH + k
-                    out[item, 0, at, :] = p_re * s_re - p_im * s_im + (q_re * d_re - q_im * d_im)
-                    out[item, 1, at, :] = p_re * s_im + p_im * s_re + (q_re * d_im + q_im * d_re)
+
+        @pl.when(upper)
+        def _():
+            for slot in range(near):
+                arrived(outs[s].at[pl.ds(slot * mper, mper)], recv_f.at[s, slot])
+
+        @pl.when(~upper)
+        def _():
+            for slot in range(near):
+                arrived(outs[s].at[pl.ds(slot * mper + 1, mper - 1)], recv_f.at[s, slot])
+                arrived(outs[s].at[pl.ds(slot * mper, 1)], recv_1.at[s, slot])
+
     for s in range(SETS):
-        for offset in range(1, gx):
-            v_copy(s, offset).wait_send()
-        for offset in range(1, count):
-            g_copy(s, lax.rem(me + offset, count)).wait_send()
-        for offset in range(1, gy):
-            f_copy(s, offset).wait_send()
+        for offset in range(gx):
+            v_ship(s, offset, False)
+        x_ship(s, False)
+        for t in range(owners):
+            g_ship(s, jnp.int32(t), False)
+
+        def sent():
+            for step in range(1, gy + 1):
+                f_ship(s, step, False)
+
+        owned(sent)
+
+        @pl.when(at_end)
+        def _():
+            for step in range(1, gy + 1):
+                e_ship(s, step, False)
 
 
 def far(sd, freqs, grid_rows, grid_cols):
     gx, gy = lax.axis_size("gx"), lax.axis_size("gy")
     count = gx * gy
-    nu, vb, nper = NA // gx, NA // gy, NA // count
-    wide = sd[0].shape[2]
+    nu, vb = NA // gx, NA // gy
+    mper, owners, near = layout(gx, gy)
+    lanes = sd[0].shape[2]
+    wide = NF * EACH * 2
     bf16 = jnp.bfloat16
     turn_re, turn_im = jnp.cos(1.5 * freqs), jnp.sin(1.5 * freqs)
     half_re, half_im = jnp.cos(0.5 * freqs), jnp.sin(0.5 * freqs)
@@ -653,22 +747,28 @@
     dma = pltpu.SemaphoreType.DMA
     done = pl.pallas_call(
         functools.partial(far_kernel, grid_rows, grid_cols),
-        out_shape=jax.ShapeDtypeStruct((NF * 4, 2, nu, vb), jnp.float32),
+        out_shape=(jax.ShapeDtypeStruct((nu, wide, vb), bf16),) * SETS,
         in_specs=[SM] + [ANY] * SETS,
-        out_specs=VM,
+        out_specs=(ANY,) * SETS,
         scratch_shapes=[
-            pltpu.VMEM((count, 2 * nper, grid_rows), bf16),
+            pltpu.VMEM((NA + 16, grid_rows), bf16),
             pltpu.VMEM((2, grid_cols, NA), bf16),
-            pltpu.VMEM((SETS, grid_rows, wide), bf16),
-            pltpu.VMEM((SETS, wide // LANES, 2 * NA, LANES), bf16),
-            pltpu.VMEM((SETS, 2 * EACH, 2 * nper, grid_cols), bf16),
-            pltpu.VMEM((SETS, gy, 2 * EACH, 2, nper, vb), bf16),
-            pltpu.VMEM((SETS, gy, 2 * EACH, 2, nper, vb), bf16),
+            pltpu.VMEM((SETS, grid_rows, lanes), bf16),
+            pltpu.VMEM((SETS, lanes // LANES, NA + 16, LANES), bf16),
+            pltpu.VMEM((SETS, 2 * EACH, 2 * mper, grid_cols), bf16),
+            pltpu.VMEM((SETS, 2 * EACH, 16, grid_cols), bf16),
+            pltpu.VMEM((SETS, gy, 2, mper, wide, vb), bf16),
+            pltpu.VMEM((SETS, gy, 1, wide, vb), bf16),
             dma((SETS, gx)),
             dma((SETS, gx)),
+            dma((SETS, owners)),
             dma((SETS, count)),
+            dma((SETS,)),
             dma((SETS, count)),
+            dma((SETS, 2, gy)),
+            dma((SETS, near)),
             dma((SETS, gy)),
+            dma((SETS, near)),
             dma((SETS, gy)),
         ],
         compiler_params=pltpu.CompilerParams(
@@ -676,7 +776,8 @@
         ),
         name="far",
     )(mix, *sd)
-    return jnp.transpose(done, (2, 0, 1, 3))
+    done = [part.astype(jnp.float32).reshape(nu, NF, EACH, 2, vb) for part in done]
+    return jnp.concatenate(done, 2).reshape(nu, NF * 4, 2, vb)
 
 
 def on_device(e_field, h_field, material, eps_table, src_pos, src_amp, freqs):

time: 131 us -> 116 us (0.89)
  Pallas kernels: 123 us -> 107 us
  other arithmetic: 1.3 us -> 5.24 us
  local copies, waits for them, and re-layouts: 4.9 us -> 2.85 us
    pallas_call x1, Pallas kernels: 88.8 us -> 73.2 us  [far(): pl.pallas_call(functools.partial(far_kernel, grid_rows, grid_cols), out_s...]
    unnamed x1 -> x0, local copies, waits for them, and re-layouts: 4.53 us -> none
    reshape x0 -> x1, other arithmetic: none -> 2.54 us  [far(): return jnp.concatenate(done, 2).reshape(nu, NF * 4, 2, vb)]
    reshape x0 -> x2, local copies, waits for them, and re-layouts: none -> 2.48 us  [far(): part.astype(jnp.float32).reshape(nu, NF, EACH, 2, vb)]
    concatenate x0 -> x1, other arithmetic: none -> 1.35 us  [far(): return jnp.concatenate(done, 2).reshape(nu, NF * 4, 2, vb)]
where the time goes in v3:
time: 116 us
  Pallas kernels  107 us (92%)
  other arithmetic  5.24 us (5%)
  local copies, waits for them, and re-layouts  2.85 us (2%)
    pallas_call x1, Pallas kernels, far(): pl.pallas_call(functools.partial(far_kernel, grid_rows, grid_cols), out_s...  73.2 us
    pallas_call x1, Pallas kernels, yee(): pl.pallas_call(functools.partial(yee_kernel, grid_rows, grid_cols, per),...  21.2 us
    pallas_call x1, Pallas kernels, halo(): pl.pallas_call(halo_kernel, out_shape=(jax.ShapeDtypeStruct((rows, LANES)...  12.6 us
    reshape x1, other arithmetic, far(): return jnp.concatenate(done, 2).reshape(nu, NF * 4, 2, vb)  2.54 us
    reshape x2, local copies, waits for them, and re-layouts, far(): part.astype(jnp.float32).reshape(nu, NF, EACH, 2, vb)  2.48 us

profile of v3, /device:TPU:0, one launch (start us, length us, event | category | flops | bytes accessed | tf_op | source)
XLA Modules:
  0.0 115.8 jit_solution(17426795159464526338)
XLA Ops:
  0.6 0.7 multiply_bitcast_fusion.3
  1.3 0.1 copy.10
  1.4 0.1 copy.11
  1.5 0.1 copy.13
  1.6 0.1 copy.12
  1.7 0.6 maximum_multiply_fusion.mix
  2.4 12.6 %halo.1 = (f32[256,128]{1,0:T(8,128)}, f32[2,8,128]{2,1,0:T(8,128)}, f32[2,18,8,512]{3,2,1,0:T(8,128)}, s32[2,3,8,512]{3,2,1,0:T(8,128)}) custom-call(f32[9,256,512]{2,1,0:T(8,128)} %bitcast.16, f32[9,256,512]{2,1,0:T(8,128)} %bitcast.18, s32[3,256,512]{2,1,0:T(8,128)} %m_hbm.1), custom_call_target="tpu_custom_call" | custom-call | tf_op jit(solution)/shard_map/halo/pallas_call | solution.py:153
  15.0 21.2 %yee.1 = (f32[9,256,512]{2,1,0:T(8,128)}, f32[9,256,512]{2,1,0:T(8,128)}, bf16[8,256,256]{2,1,0:T(8,128)(2,1)}, bf16[8,256,256]{2,1,0:T(8,128)(2,1)}) custom-call(f32[9,256,512]{2,1,0:T(8,128)} %bitcast.17, f32[9,256,512]{2,1,0:T(8,128)} %bitcast.19, s32[3,256,512]{2,1,0:T(8,128)} %m_hbm.1, f32[256,128]{1,0:T(8,128)} %get-tuple-element.13.col_rim, ...), custom_call_target="tpu_custom_call" | custom-call | tf_op jit(solution)/shard_map/yee/pallas_call | solution.py:387
  36.2 73.2 %far.1 = (bf16[128,8,256]{2,1,0:T(8,128)(2,1)}, bf16[128,8,256]{2,1,0:T(8,128)(2,1)}) custom-call(f32[2,4]{1,0:T(2,128)} %maximum_multiply_fusion.mix, bf16[8,256,256]{2,1,0:T(8,128)(2,1)} %get-tuple-element.19.rest_0_, bf16[8,256,256]{2,1,0:T(8,128)(2,1)} %get-tuple-element.20.rest_1_), custom_call_target="tpu_custom_call" | custom-call | tf_op jit(solution)/shard_map/far/pallas_call | solution.py:748
  109.4 1.2 %reshape.36 = bf16[128,2,2,2,256]{4,3,2,1,0:T(2,128)(2,1)S(1)} reshape(bf16[128,8,256]{2,1,0:T(8,128)(2,1)} %get-tuple-element.21) | data formatting | bytes 1048576 | tf_op jit(solution)/shard_map/reshape | solution.py:779
  110.7 1.2 %reshape.37 = bf16[128,2,2,2,256]{4,3,2,1,0:T(2,128)(2,1)S(1)} reshape(bf16[128,8,256]{2,1,0:T(8,128)(2,1)} %get-tuple-element.22) | data formatting | bytes 1048576 | tf_op jit(solution)/shard_map/reshape | solution.py:779
  111.9 1.4 %pad_maximum_fusion = bf16[128,2,4,2,256]{4,3,2,1,0:T(2,128)(2,1)S(1)} fusion(bf16[128,2,2,2,256]{4,3,2,1,0:T(2,128)(2,1)S(1)} %reshape.37, bf16[128,2,2,2,256]{4,3,2,1,0:T(2,128)(2,1)S(1)} %reshape.36), kind=kLoop, calls=%fused_computation | loop fusion | flops 524288 | bytes 2097152 | tf_op jit(solution)/shard_map/concatenate | solution.py:780
  113.3 2.5 %convert.4 = f32[128,8,2,256]{3,2,1,0:T(2,128)} convert(bf16[128,8,2,256]{3,2,1,0:T(2,128)(2,1)S(1)} %bitcast.20) | non-fusion elementwise | flops 524288 | bytes 3145728 | tf_op jit(solution)/shard_map/reshape | solution.py:780

commit v4 on v3

--- a/solution.py
+++ b/solution.py
@@ -201,32 +201,54 @@
     for copy in copies:
         copy.start()
     count = amp.shape[1]
-    step = min(count, 1024)
     used = high - 2 * CHUNK
-    row_at = row0 + lax.broadcasted_iota(jnp.int32, (used, step), 0) + (CHUNK - BASE)
-    lane = lax.broadcasted_iota(jnp.int32, (width, step), 0)
-    col_at = col0 + jnp.where(lane < cols + PAD // 2, lane, lane - width)
-    for start in range(0, count, step):
-        at = pl.ds(start, step)
-        amp_now = amp[:, at]
-        hi = amp_now.astype(jnp.bfloat16).astype(jnp.float32)
-        mid = (amp_now - hi).astype(jnp.bfloat16).astype(jnp.float32)
-        low = amp_now - hi - mid
-        hit_col = jnp.where(col_at == pos[2:3, at], 1.0, 0.0).astype(jnp.bfloat16)
-        hit_row = row_at == pos[1:2, at]
+    bf16 = jnp.bfloat16
+    gather = functools.partial(
+        lax.dot_general, dimension_numbers=(((1,), (1,)), ((), ())), preferred_element_type=jnp.float32
+    )
+    tall_at = lambda shape: row0 + lax.broadcasted_iota(jnp.int32, shape, 0) + (CHUNK - BASE)
+    lane = lax.broadcasted_iota(jnp.int32, (width, LANES), 0)
+    col_at = (col0 + jnp.where(lane < cols + PAD // 2, lane, lane - width)).astype(jnp.float32)
+    row_at = tall_at((used, LANES)).astype(jnp.float32)
+    row_s = jnp.broadcast_to(pos[1:2, :], (8, count))
+    col_s = jnp.broadcast_to(pos[2:3, :], (8, count))
+    inside = (row_s >= row0 - (BASE - CHUNK)) & (row_s < row0 + used - (BASE - CHUNK))
+    inside &= (col_s >= col0 - PAD // 2) & (col_s < col0 + cols + PAD // 2)
+    rank = jnp.where(inside, 1.0, 0.0)
+    at_lane = lax.broadcasted_iota(jnp.int32, (8, count), 1)
+    reach = 1
+    while reach < count:
+        rank = rank + jnp.where(at_lane >= reach, pltpu.roll(rank, reach, 1), 0.0)
+        reach *= 2
+    found = jnp.max(rank).astype(jnp.int32)
+    rank = jnp.where(inside, rank, 0.0)[:1]
+    hi = amp[...].astype(bf16).astype(jnp.float32)
+    mid = (amp[...] - hi).astype(bf16).astype(jnp.float32)
+    low = amp[...] - hi - mid
+    parts = [
+        (pos[1:2, :] >> 6).astype(jnp.float32), (pos[1:2, :] & 63).astype(jnp.float32),
+        (pos[2:3, :] >> 6).astype(jnp.float32), (pos[2:3, :] & 63).astype(jnp.float32),
+        pos[0:1, :].astype(jnp.float32), hi, mid, low,
+    ]
+    parts = jnp.concatenate(parts, 0).astype(bf16)
+    for layer in range(LZ):
+        src[layer] = jnp.zeros((high, width), jnp.float32)
+    slot = lax.broadcasted_iota(jnp.int32, (LANES, count), 0).astype(jnp.float32)
+
+    def place(group, carry):
+        pick = jnp.where(slot + (group * LANES + 1).astype(jnp.float32) == rank, 1.0, 0.0)
+        some = gather(parts, pick.astype(bf16))
+        row, col = some[0:1] * 64.0 + some[1:2], some[2:3] * 64.0 + some[3:4]
+        hit_col = jnp.where(col_at == col, 1.0, 0.0).astype(bf16)
+        hit_col = jnp.concatenate([hit_col] * 3, 1)
+        hit_row = row_at == row
         for layer in range(LZ):
-            hit = hit_row & (pos[0:1, at] == layer)
-            total = None
-            for piece in (hi, mid, low):
-                left = jnp.where(hit, piece, 0.0).astype(jnp.bfloat16)
-                term = lax.dot_general(
-                    left, hit_col, (((1,), (1,)), ((), ())), preferred_element_type=jnp.float32
-                )
-                total = term if total is None else total + term
-            if start == 0:
-                src[layer, CHUNK : CHUNK + used, :] = total
-            else:
-                src[layer, CHUNK : CHUNK + used, :] += total
+            hit = hit_row & (some[4:5] == float(layer))
+            left = [jnp.where(hit, some[p : p + 1], 0.0).astype(bf16) for p in (5, 6, 7)]
+            src[layer, CHUNK : CHUNK + used, :] += gather(jnp.concatenate(left, 1), hit_col)
+        return carry
+
+    lax.fori_loop(0, lax.div(found + (LANES - 1), LANES), place, 0)
     copies[2].wait()
 
     def scale_of(index, row, col):
@@ -442,7 +464,7 @@
     return mper, NA // 2 // mper, NA // gx // mper
 
 
-def far_kernel(grid_rows, grid_cols, mix, *rest):
+def far_kernel(grid_rows, grid_cols, freqs, *rest):
     sd, outs, rest = rest[:SETS], rest[SETS : 2 * SETS], rest[2 * SETS :]
     x_tab, y_tab, v, g, left, left_x, held, held_x, *sems = rest
     send_v, recv_v, send_g, recv_g, send_x, recv_x, send_f, recv_f, send_1, recv_1, send_e = sems
@@ -592,6 +614,15 @@
 
         lax.fori_loop(0, grid_cols // tall, body, 0)
 
+    inv_norm = 1.0 / math.sqrt(grid_rows * grid_cols)
+    mix = []
+    for f in range(NF):
+        angle = jnp.full((8, LANES), 0.5 * freqs[f], jnp.float32)
+        half_re, half_im = jnp.cos(angle), jnp.sin(angle)
+        turn_re, turn_im = jnp.cos(3.0 * angle) * inv_norm, jnp.sin(3.0 * angle) * inv_norm
+        four = (turn_re * half_re, turn_im * half_re, -turn_im * half_im, turn_re * half_im)
+        mix.append([value[:1, :1] for value in four])
+
     dot = functools.partial(jnp.dot, preferred_element_type=jnp.float32)
     parts = 2
     group = owners // parts
@@ -643,7 +674,7 @@
 
         fields = [both_signs(f) for f in range(2 * EACH)]
         for f in range(NF):
-            p0, p1, q0, q1 = (mix[f, t] for t in range(4))
+            p0, p1, q0, q1 = mix[f]
             for k in range(EACH):
                 for sign, result in enumerate((plus, minus)):
                     s_re, s_im = fields[k][sign]
@@ -731,6 +762,16 @@
                 e_ship(s, step, False)
 
 
+def order_kernel(*refs):
+    *parts, out = refs
+    for s, part in enumerate(parts):
+        block = part[...].astype(jnp.float32)
+        for f in range(NF):
+            for k in range(EACH):
+                at = 2 * (f * EACH + k)
+                out[:, f * 4 + s * EACH + k] = block[:, at : at + 2]
+
+
 def far(sd, freqs, grid_rows, grid_cols):
     gx, gy = lax.axis_size("gx"), lax.axis_size("gy")
     count = gx * gy
@@ -739,11 +780,6 @@
     lanes = sd[0].shape[2]
     wide = NF * EACH * 2
     bf16 = jnp.bfloat16
-    turn_re, turn_im = jnp.cos(1.5 * freqs), jnp.sin(1.5 * freqs)
-    half_re, half_im = jnp.cos(0.5 * freqs), jnp.sin(0.5 * freqs)
-    mix = jnp.stack(
-        [turn_re * half_re, turn_im * half_re, -turn_im * half_im, turn_re * half_im], 1
-    ) * (1.0 / math.sqrt(grid_rows * grid_cols))
     dma = pltpu.SemaphoreType.DMA
     done = pl.pallas_call(
         functools.partial(far_kernel, grid_rows, grid_cols),
@@ -775,9 +811,16 @@
             vmem_limit_bytes=BIG, collective_id=1, has_side_effects=True
         ),
         name="far",
-    )(mix, *sd)
-    done = [part.astype(jnp.float32).reshape(nu, NF, EACH, 2, vb) for part in done]
-    return jnp.concatenate(done, 2).reshape(nu, NF * 4, 2, vb)
+    )(freqs, *sd)
+    block = nu // 4
+    return pl.pallas_call(
+        order_kernel,
+        grid=(4,),
+        out_shape=jax.ShapeDtypeStruct((nu, NF * 4, 2, vb), jnp.float32),
+        in_specs=[pl.BlockSpec((block, wide, vb), lambda n: (n, 0, 0))] * SETS,
+        out_specs=pl.BlockSpec((block, NF * 4, 2, vb), lambda n: (n, 0, 0, 0)),
+        name="order",
+    )(*done)
 
 
 def on_device(e_field, h_field, material, eps_table, src_pos, src_amp, freqs):

time: 116 us -> 112 us (0.966)
  other arithmetic: 5.24 us -> 0 us
  Pallas kernels: 107 us -> 111 us
  local copies, waits for them, and re-layouts: 2.85 us -> 0 us
    pallas_call x0 -> x1, Pallas kernels: none -> 3.8 us  [far(): pl.pallas_call(order_kernel, grid=(4,), out_shape=jax.ShapeDtypeStruct((n...]
    reshape x1 -> x0, other arithmetic: 2.54 us -> none  [far(): return jnp.concatenate(done, 2).reshape(nu, NF * 4, 2, vb)]
    reshape x2 -> x0, local copies, waits for them, and re-layouts: 2.48 us -> none  [far(): part.astype(jnp.float32).reshape(nu, NF, EACH, 2, vb)]
    concatenate x1 -> x0, other arithmetic: 1.35 us -> none  [far(): return jnp.concatenate(done, 2).reshape(nu, NF * 4, 2, vb)]
where the time goes in v4:
time: 112 us; the launch traced here: 111 us
  Pallas kernels  111 us (99%)
    pallas_call x1, Pallas kernels, far(): pl.pallas_call(functools.partial(far_kernel, grid_rows, grid_cols), out_s...  73.2 us
    pallas_call x1, Pallas kernels, yee(): pl.pallas_call(functools.partial(yee_kernel, grid_rows, grid_cols, per),...  21.2 us
    pallas_call x1, Pallas kernels, halo(): pl.pallas_call(halo_kernel, out_shape=(jax.ShapeDtypeStruct((rows, LANES)...  12.7 us
    pallas_call x1, Pallas kernels, far(): pl.pallas_call(order_kernel, grid=(4,), out_shape=jax.ShapeDtypeStruct((n...  3.8 us

profile of v4, /device:TPU:0, one launch (start us, length us, event | category | flops | bytes accessed | tf_op | source)
XLA Modules:
  0.0 111.5 jit_solution(8594347870967586453)
XLA Ops:
  0.6 12.7 %halo.1 = (f32[256,128]{1,0:T(8,128)}, f32[2,8,128]{2,1,0:T(8,128)}, f32[2,18,8,512]{3,2,1,0:T(8,128)}, s32[2,3,8,512]{3,2,1,0:T(8,128)}) custom-call(f32[9,256,512]{2,1,0:T(8,128)} %bitcast.6, f32[9,256,512]{2,1,0:T(8,128)} %bitcast.8, s32[3,256,512]{2,1,0:T(8,128)} %m_hbm.1), custom_call_target="tpu_custom_call" | custom-call | tf_op jit(solution)/shard_map/halo/pallas_call | solution.py:153
  13.3 21.2 %yee.1 = (f32[9,256,512]{2,1,0:T(8,128)}, f32[9,256,512]{2,1,0:T(8,128)}, bf16[8,256,256]{2,1,0:T(8,128)(2,1)}, bf16[8,256,256]{2,1,0:T(8,128)(2,1)}) custom-call(f32[9,256,512]{2,1,0:T(8,128)} %bitcast.7, f32[9,256,512]{2,1,0:T(8,128)} %bitcast.9, s32[3,256,512]{2,1,0:T(8,128)} %m_hbm.1, f32[256,128]{1,0:T(8,128)} %get-tuple-element.13.col_rim, ...), custom_call_target="tpu_custom_call" | custom-call | tf_op jit(solution)/shard_map/yee/pallas_call | solution.py:409
  34.5 73.2 %far.1 = (bf16[128,8,256]{2,1,0:T(8,128)(2,1)}, bf16[128,8,256]{2,1,0:T(8,128)(2,1)}) custom-call(f32[2]{0:T(128)} %freqs.1, bf16[8,256,256]{2,1,0:T(8,128)(2,1)} %get-tuple-element.19.rest_0_, bf16[8,256,256]{2,1,0:T(8,128)(2,1)} %get-tuple-element.20.rest_1_), custom_call_target="tpu_custom_call" | custom-call | tf_op jit(solution)/shard_map/far/pallas_call | solution.py:784
  107.7 3.8 %order.1 = f32[128,8,2,256]{3,2,1,0:T(2,128)} custom-call(bf16[128,8,256]{2,1,0:T(8,128)(2,1)} %get-tuple-element.21.refs_0_, bf16[128,8,256]{2,1,0:T(8,128)(2,1)} %get-tuple-element.22.refs_1_), custom_call_target="tpu_custom_call" | custom-call | tf_op jit(solution)/shard_map/order/pallas_call | solution.py:816

commit v5 on v4

--- a/solution.py
+++ b/solution.py
@@ -21,6 +21,7 @@
 
 BASE = 32
 CHUNK = 16
+PAIR = 32
 SETS = 2
 EACH = 4 // SETS
 LANES = 128
@@ -186,20 +187,35 @@
     e_hbm, h_hbm, m_hbm, col_rim, corner, rim_f, rim_m, eps, pos, amp,
     e_out, h_out, *rest,
 ):
-    sd_outs, (e_ext, h_ext, m_main, scale, src, first, sems) = rest[:SETS], rest[SETS:]
+    sd_outs, (e_ext, h_ext, m_main, scale, src, first, *sd, sems) = rest[:SETS], rest[SETS:]
     rows, cols = m_main.shape[1:]
     width = cols + PAD
     high = e_ext.shape[1]
     row0 = lax.axis_index("gx") * rows
     col0 = lax.axis_index("gy") * cols
-    main_r = pl.ds(BASE, rows)
-    copies = [
-        pltpu.make_async_copy(e_hbm, e_ext.at[:, main_r, pl.ds(0, cols)], sems.at[0]),
-        pltpu.make_async_copy(h_hbm, h_ext.at[:, main_r, pl.ds(0, cols)], sems.at[1]),
-        pltpu.make_async_copy(m_hbm, m_main, sems.at[2]),
-    ]
-    for copy in copies:
-        copy.start()
+    pairs = rows // PAIR
+
+    def load(q):
+        here, there = pl.ds(PAIR * q, PAIR), pl.ds(BASE + PAIR * q, PAIR)
+        return [
+            pltpu.make_async_copy(e_hbm.at[:, here, :], e_ext.at[:, there, pl.ds(0, cols)], sems.at[0, q]),
+            pltpu.make_async_copy(h_hbm.at[:, here, :], h_ext.at[:, there, pl.ds(0, cols)], sems.at[1, q]),
+            pltpu.make_async_copy(m_hbm.at[:, here, :], m_main.at[:, here, :], sems.at[2, q]),
+        ]
+
+    def store(q):
+        here, there = pl.ds(PAIR * q, PAIR), pl.ds(BASE + PAIR * q, PAIR)
+        return [
+            pltpu.make_async_copy(e_ext.at[:, there, pl.ds(0, cols)], e_out.at[:, here, :], sems.at[3, q]),
+            pltpu.make_async_copy(h_ext.at[:, there, pl.ds(0, cols)], h_out.at[:, here, :], sems.at[4, q]),
+        ] + [
+            pltpu.make_async_copy(sd[s].at[:, here, :], sd_outs[s].at[:, here, :], sems.at[5 + s, q])
+            for s in range(SETS)
+        ]
+
+    for q in range(pairs):
+        for copy in load(q):
+            copy.start()
     count = amp.shape[1]
     used = high - 2 * CHUNK
     bf16 = jnp.bfloat16
@@ -249,7 +265,6 @@
         return carry
 
     lax.fori_loop(0, lax.div(found + (LANES - 1), LANES), place, 0)
-    copies[2].wait()
 
     def scale_of(index, row, col):
         value = jnp.full(index.shape, eps[0], jnp.float32)
@@ -281,7 +296,6 @@
             h_ext[plane, far, cols:] = shown(block, 3 * LZ + plane)
         return carry
 
-    lax.fori_loop(0, rows // CHUNK, fill, 0)
     row_eight = row0 + lax.broadcasted_iota(jnp.int32, (8, cols), 0)
     blank = jnp.zeros((8, width), jnp.float32)
     for side, target, offset, spare in (
@@ -312,8 +326,6 @@
     col_c = col0 + jnp.where(lane_c < cols + PAD // 2, lane_c, lane_c - width)
     weight = jnp.where(col_c >= 0, courant, 0.0)
     top = lax.axis_index("gx") == 0
-    copies[0].wait()
-    copies[1].wait()
 
     def magnetic_pass(index, carry):
         r = pl.multiple_of(index * CHUNK, CHUNK)
@@ -373,24 +385,45 @@
                             for q in range(cols // LANES):
                                 piece = value[:, q * LANES : (q + 1) * LANES].astype(jnp.bfloat16)
                                 lanes = pl.ds(place * LANES, LANES)
-                                sd_outs[item // EACH][q * (2 * EACH // per) + share, here, lanes] = piece
+                                sd[item // EACH][q * (2 * EACH // per) + share, here, lanes] = piece
                     else:
                         first[item, now, :] = face
         return carry
 
-    chunks = high // CHUNK
-    main0 = BASE // CHUNK
-    main1 = main0 + rows // CHUNK
-    lax.fori_loop(1, chunks - 1, magnetic_pass, 0)
-    lax.fori_loop(1, chunks - 1, functools.partial(electric_pass, 1.0, False), 0)
-    lax.fori_loop(1, main1, magnetic_pass, 0)
-    out_h = pltpu.make_async_copy(h_ext.at[:, main_r, pl.ds(0, cols)], h_out, sems.at[3])
-    out_h.start()
-    lax.fori_loop(main0, main1, functools.partial(electric_pass, 2.0, True), 0)
-    out_e = pltpu.make_async_copy(e_ext.at[:, main_r, pl.ds(0, cols)], e_out, sems.at[4])
-    out_e.start()
-    out_h.wait()
-    out_e.wait()
+    def arrive(q):
+        for copy in load(q):
+            copy.wait()
+        for part in range(PAIR // CHUNK):
+            fill(q * (PAIR // CHUNK) + part, 0)
+
+    def advance(n, second):
+        magnetic_pass(n, 0)
+        electric_pass(1.0, False, n, 0)
+        magnetic_pass(n - 1, 0)
+        if second:
+            electric_pass(2.0, True, n - 1, 0)
+
+    start = BASE // CHUNK
+    arrive(0)
+    magnetic_pass(start - 1, 0)
+    electric_pass(1.0, False, start - 1, 0)
+    advance(start, False)
+
+    def wave(q, carry):
+        @pl.when(q < pairs - 1)
+        def _():
+            arrive(q + 1)
+
+        for part in range(PAIR // CHUNK):
+            advance(start + 1 + q * (PAIR // CHUNK) + part, True)
+        for copy in store(q):
+            copy.start()
+        return carry
+
+    lax.fori_loop(0, pairs, wave, 0)
+    for q in range(pairs):
+        for copy in store(q):
+            copy.wait()
 
 
 def yee(e_field, h_field, material, eps_table, src_pos, src_amp):
@@ -414,7 +447,7 @@
         )
         + (jax.ShapeDtypeStruct((gx, rows, per * LANES), jnp.bfloat16),) * SETS,
         in_specs=[ANY, ANY, ANY, VM, VM, VM, VM, SM, VM, VM],
-        out_specs=(ANY, ANY) + (VM,) * SETS,
+        out_specs=(ANY,) * (2 + SETS),
         scratch_shapes=[
             pltpu.VMEM((planes, high, width), f32),
             pltpu.VMEM((planes, high, width), f32),
@@ -422,7 +455,10 @@
             pltpu.VMEM((LZ, high, width), f32),
             pltpu.VMEM((LZ, high, width), f32),
             pltpu.VMEM((4, high, width), f32),
-            pltpu.SemaphoreType.DMA((5,)),
+        ]
+        + [pltpu.VMEM((gx, rows, per * LANES), jnp.bfloat16)] * SETS
+        + [
+            pltpu.SemaphoreType.DMA((5 + SETS, rows // PAIR)),
         ],
         compiler_params=pltpu.CompilerParams(vmem_limit_bytes=BIG),
         name="yee",

time: 112 us -> 106 us (0.946)
  Pallas kernels: 111 us -> 105 us
    pallas_call x1, Pallas kernels: 21.2 us -> 15.7 us  [yee(): pl.pallas_call(functools.partial(yee_kernel, grid_rows, grid_cols, per),...]
where the time goes in v5:
time: 106 us
  Pallas kernels  105 us (99%)
    pallas_call x1, Pallas kernels, far(): pl.pallas_call(functools.partial(far_kernel, grid_rows, grid_cols), out_s...  73.2 us
    pallas_call x1, Pallas kernels, yee(): pl.pallas_call(functools.partial(yee_kernel, grid_rows, grid_cols, per),...  15.7 us
    pallas_call x1, Pallas kernels, halo(): pl.pallas_call(halo_kernel, out_shape=(jax.ShapeDtypeStruct((rows, LANES)...  12.7 us
    pallas_call x1, Pallas kernels, far(): pl.pallas_call(order_kernel, grid=(4,), out_shape=jax.ShapeDtypeStruct((n...  3.8 us

profile of v5, /device:TPU:0, one launch (start us, length us, event | category | flops | bytes accessed | tf_op | source)
XLA Modules:
  0.0 106.0 jit_solution(9924490351718922309)
XLA Ops:
  0.6 12.7 %halo.1 = (f32[256,128]{1,0:T(8,128)}, f32[2,8,128]{2,1,0:T(8,128)}, f32[2,18,8,512]{3,2,1,0:T(8,128)}, s32[2,3,8,512]{3,2,1,0:T(8,128)}) custom-call(f32[9,256,512]{2,1,0:T(8,128)} %bitcast.6, f32[9,256,512]{2,1,0:T(8,128)} %bitcast.8, s32[3,256,512]{2,1,0:T(8,128)} %m_hbm.1), custom_call_target="tpu_custom_call" | custom-call | tf_op jit(solution)/shard_map/halo/pallas_call | solution.py:154
  13.3 15.7 %yee.1 = (f32[9,256,512]{2,1,0:T(8,128)}, f32[9,256,512]{2,1,0:T(8,128)}, bf16[8,256,256]{2,1,0:T(8,128)(2,1)}, bf16[8,256,256]{2,1,0:T(8,128)(2,1)}) custom-call(f32[9,256,512]{2,1,0:T(8,128)} %bitcast.7, f32[9,256,512]{2,1,0:T(8,128)} %bitcast.9, s32[3,256,512]{2,1,0:T(8,128)} %m_hbm.1, f32[256,128]{1,0:T(8,128)} %get-tuple-element.13.col_rim, ...), custom_call_target="tpu_custom_call" | custom-call | tf_op jit(solution)/shard_map/yee/pallas_call | solution.py:442
  29.0 73.2 %far.1 = (bf16[128,8,256]{2,1,0:T(8,128)(2,1)}, bf16[128,8,256]{2,1,0:T(8,128)(2,1)}) custom-call(f32[2]{0:T(128)} %freqs.1, bf16[8,256,256]{2,1,0:T(8,128)(2,1)} %get-tuple-element.19.rest_0_, bf16[8,256,256]{2,1,0:T(8,128)(2,1)} %get-tuple-element.20.rest_1_), custom_call_target="tpu_custom_call" | custom-call | tf_op jit(solution)/shard_map/far/pallas_call | solution.py:820
  102.2 3.8 %order.1 = f32[128,8,2,256]{3,2,1,0:T(2,128)} custom-call(bf16[128,8,256]{2,1,0:T(8,128)(2,1)} %get-tuple-element.21.refs_0_, bf16[128,8,256]{2,1,0:T(8,128)(2,1)} %get-tuple-element.22.refs_1_), custom_call_target="tpu_custom_call" | custom-call | tf_op jit(solution)/shard_map/order/pallas_call | solution.py:852

commit v6 on v5

--- a/solution.py
+++ b/solution.py
@@ -22,9 +22,16 @@
 BASE = 32
 CHUNK = 16
 PAIR = 32
-SETS = 2
-EACH = 4 // SETS
 LANES = 128
+Y_STEPS = 8
+Y_EARLY = 2
+ORDER = {
+    2: ("a0", "a1", "x0", "r0", "y2", "y3", "y4", "y5", "y6", "y7", "r1", "c0", "c1"),
+    4: (
+        "a0", "a1", "x0", "r0", "a2", "y2", "y3", "r1", "a3", "y4",
+        "y5", "y6", "y7", "c0", "r2", "c1", "r3", "c2", "c3",
+    ),
+}
 PAD = 128
 ANY = pl.BlockSpec(memory_space=pl.ANY)
 VM = pl.BlockSpec(memory_space=pltpu.VMEM)
@@ -74,12 +81,12 @@
         return step, copy
 
     rows_out, cols_out = [], []
-    for side, low in enumerate((0, rows - 8)):
+    for side, low in enumerate((0, rows - 2)):
         step = (2 * side - 1, 0)
-        at = pl.ds(low, 8)
-        rows_out.append(remote(step, e.at[:, at, :], got_f.at[side, pl.ds(0, planes)], 3 * side))
-        rows_out.append(remote(step, h.at[:, at, :], got_f.at[side, pl.ds(planes, planes)], 3 * side + 1))
-        rows_out.append(remote(step, m.at[:, at, :], got_m.at[side], 3 * side + 2))
+        at, to = pl.ds(low, 2), pl.ds(6 * side, 2)
+        rows_out.append(remote(step, e.at[:, at, :], got_f.at[side, pl.ds(0, planes), to], 3 * side))
+        rows_out.append(remote(step, h.at[:, at, :], got_f.at[side, pl.ds(planes, planes), to], 3 * side + 1))
+        rows_out.append(remote(step, m.at[:, at, :], got_m.at[side, :, to], 3 * side + 2))
     for side in range(2):
         cols_out.append(remote((0, 2 * side - 1), packed.at[side], got_col.at[side], 6 + side))
         for end, low in enumerate((0, rows - 8)):
@@ -135,8 +142,10 @@
     lax.fori_loop(0, rows // tall, merge, 0)
     for side in range(2):
         there = exists((1 - 2 * side, 0))
-        rim_f[side] = jnp.where(there, got_f[side], 0.0)
-        rim_m[side] = jnp.where(there, got_m[side], 0)
+        row = lax.broadcasted_iota(jnp.int32, (8, cols), 0)
+        kept = there & ((row >= 6) if side else (row < 2))
+        rim_f[side] = jnp.where(kept[None], got_f[side], 0.0)
+        rim_m[side] = jnp.where(kept[None], got_m[side], 0)
         right = jnp.where(there & after, got_corner[side, 0], 0.0)
         left = jnp.where(there & before, got_corner[side, 1], 0.0)
         corner[side] = jnp.where(last[:8], right, left)
@@ -178,16 +187,19 @@
     )(e, h, m)
 
 
-def fields_per_device(gx, cols):
-    return 2 * EACH * cols // (gx * LANES)
+def split_sets(gx, cols):
+    sets = 4 if 2 * cols >= gx * LANES else 2
+    each = 4 // sets
+    return sets, each, 2 * each * cols // (gx * LANES)
 
 
 def yee_kernel(
-    grid_rows, grid_cols, per,
+    grid_rows, grid_cols, plan,
     e_hbm, h_hbm, m_hbm, col_rim, corner, rim_f, rim_m, eps, pos, amp,
     e_out, h_out, *rest,
 ):
-    sd_outs, (e_ext, h_ext, m_main, scale, src, first, *sd, sems) = rest[:SETS], rest[SETS:]
+    sets, each, per = plan
+    sd_outs, (e_ext, h_ext, m_main, scale, src, first, *sd, sems) = rest[:sets], rest[sets:]
     rows, cols = m_main.shape[1:]
     width = cols + PAD
     high = e_ext.shape[1]
@@ -210,7 +222,7 @@
             pltpu.make_async_copy(h_ext.at[:, there, pl.ds(0, cols)], h_out.at[:, here, :], sems.at[4, q]),
         ] + [
             pltpu.make_async_copy(sd[s].at[:, here, :], sd_outs[s].at[:, here, :], sems.at[5 + s, q])
-            for s in range(SETS)
+            for s in range(sets)
         ]
 
     for q in range(pairs):
@@ -381,11 +393,11 @@
                         old = first[item, now, :]
                         here = pl.ds(r - BASE, CHUNK)
                         for which, value in enumerate((old + face, face - old)):
-                            share, place = divmod(which * EACH + item % EACH, per)
+                            share, place = divmod(which * each + item % each, per)
                             for q in range(cols // LANES):
                                 piece = value[:, q * LANES : (q + 1) * LANES].astype(jnp.bfloat16)
                                 lanes = pl.ds(place * LANES, LANES)
-                                sd[item // EACH][q * (2 * EACH // per) + share, here, lanes] = piece
+                                sd[item // each][q * (2 * each // per) + share, here, lanes] = piece
                     else:
                         first[item, now, :] = face
         return carry
@@ -429,7 +441,7 @@
 def yee(e_field, h_field, material, eps_table, src_pos, src_amp):
     rows, cols = material.shape[1:]
     gx = lax.axis_size("gx")
-    per = fields_per_device(gx, cols)
+    sets, each, per = split_sets(gx, cols)
     grid_rows = rows * gx
     grid_cols = cols * lax.axis_size("gy")
     planes = 3 * LZ
@@ -440,14 +452,14 @@
     width = cols + PAD
     f32 = jnp.float32
     out = pl.pallas_call(
-        functools.partial(yee_kernel, grid_rows, grid_cols, per),
+        functools.partial(yee_kernel, grid_rows, grid_cols, (sets, each, per)),
         out_shape=(
             jax.ShapeDtypeStruct((planes, rows, cols), f32),
             jax.ShapeDtypeStruct((planes, rows, cols), f32),
         )
-        + (jax.ShapeDtypeStruct((gx, rows, per * LANES), jnp.bfloat16),) * SETS,
+        + (jax.ShapeDtypeStruct((gx, rows, per * LANES), jnp.bfloat16),) * sets,
         in_specs=[ANY, ANY, ANY, VM, VM, VM, VM, SM, VM, VM],
-        out_specs=(ANY,) * (2 + SETS),
+        out_specs=(ANY,) * (2 + sets),
         scratch_shapes=[
             pltpu.VMEM((planes, high, width), f32),
             pltpu.VMEM((planes, high, width), f32),
@@ -456,9 +468,9 @@
             pltpu.VMEM((LZ, high, width), f32),
             pltpu.VMEM((4, high, width), f32),
         ]
-        + [pltpu.VMEM((gx, rows, per * LANES), jnp.bfloat16)] * SETS
+        + [pltpu.VMEM((gx, rows, per * LANES), jnp.bfloat16)] * sets
         + [
-            pltpu.SemaphoreType.DMA((5 + SETS, rows // PAIR)),
+            pltpu.SemaphoreType.DMA((5 + sets, rows // PAIR)),
         ],
         compiler_params=pltpu.CompilerParams(vmem_limit_bytes=BIG),
         name="yee",
@@ -500,115 +512,9 @@
     return mper, NA // 2 // mper, NA // gx // mper
 
 
-def far_kernel(grid_rows, grid_cols, freqs, *rest):
-    sd, outs, rest = rest[:SETS], rest[SETS : 2 * SETS], rest[2 * SETS :]
-    x_tab, y_tab, v, g, left, left_x, held, held_x, *sems = rest
-    send_v, recv_v, send_g, recv_g, send_x, recv_x, send_f, recv_f, send_1, recv_1, send_e = sems
-    gx, gy = lax.axis_size("gx"), lax.axis_size("gy")
-    i, z = lax.axis_index("gx"), lax.axis_index("gy")
-    me = i * gy + z
-    count = gx * gy
-    rows = grid_rows // gx
-    cols = grid_cols // gy
-    per = v.shape[2] // LANES
-    split = 2 * EACH // per
-    slabs = cols // LANES
-    mper, owners, near = layout(gx, gy)
+def build_x(x_tab, mper, owners):
+    grid_rows = x_tab.shape[1]
     own = 2 * mper
-    vb = NA // gy
-    wide = NF * EACH * 2
-    half = gx // 2
-    mesh_id = pl.DeviceIdType.MESH
-
-    upper = i >= half
-    plane = jnp.where(upper, i - half, half - 1 - i)
-    turn = jnp.where(upper, 0, gy) + z
-    block_id = plane * near + turn
-
-    def owner(t):
-        c, r = lax.div(t, near), lax.rem(t, near)
-        return jnp.where(r < gy, half + c, half - 1 - c), lax.rem(r, gy)
-
-    end_i, end_z = owner(jnp.int32(owners - 1))
-
-    def ship(src, dst, where, send_sem, recv_sem, start):
-        here = (where[0] == i) & (where[1] == z)
-
-        @pl.when(~here)
-        def _():
-            copy = pltpu.make_async_remote_copy(
-                src_ref=src, dst_ref=dst, send_sem=send_sem, recv_sem=recv_sem,
-                device_id=where, device_id_type=mesh_id,
-            )
-            if start:
-                copy.start()
-            else:
-                copy.wait_send()
-
-        if start:
-
-            @pl.when(here)
-            def _():
-                pltpu.make_async_copy(src, dst, recv_sem).start()
-
-    def arrived(ref, sem):
-        pltpu.make_async_copy(ref, ref, sem).wait()
-
-    barrier = pltpu.get_barrier_semaphore()
-    for offset in range(1, count):
-        peer = lax.rem(me + offset, count)
-        pl.semaphore_signal(
-            barrier, inc=1, device_id=(lax.div(peer, gy), lax.rem(peer, gy)), device_id_type=mesh_id
-        )
-    pl.semaphore_wait(barrier, count - 1)
-
-    def v_ship(s, offset, start):
-        peer = lax.rem(i + offset, gx)
-        here = pl.ds(pl.multiple_of(i * rows, rows), rows)
-        ship(sd[s].at[peer], v.at[s, here], (peer, z), send_v.at[s, offset], recv_v.at[s, i], start)
-
-    def g_ship(s, t, start):
-        lane = pl.multiple_of((z * slabs + lax.div(i, split)) * LANES, LANES)
-        to = (pl.ds(lax.rem(i, split) * per, per), slice(None), pl.ds(lane, LANES))
-        part = g.at[s, :, pl.ds(pl.multiple_of(t * own, own), own), :]
-        ship(part, left.at[(s, *to)], owner(t), send_g.at[s, t], recv_g.at[s, me], start)
-
-    def x_ship(s, start):
-        lane = pl.multiple_of((z * slabs + lax.div(i, split)) * LANES, LANES)
-        to = (pl.ds(lax.rem(i, split) * per, per), slice(None), pl.ds(lane, LANES))
-        part = g.at[s, :, pl.ds(owners * own, 16), :]
-        ship(part, left_x.at[(s, *to)], (end_i, end_z), send_x.at[s], recv_x.at[s, me], start)
-
-    def f_ship(s, step, start):
-        peer = lax.rem(z + step, gy)
-        at = pl.ds(pl.multiple_of(turn * mper, mper), mper)
-        ship(
-            held.at[s, peer, 0], outs[s].at[at], (half + plane, peer),
-            send_f.at[s, 0, step - 1], recv_f.at[s, turn], start,
-        )
-        mirror = near - 1 - turn
-        at = pl.ds(mirror * mper + 1, mper - 1)
-        ship(
-            held.at[s, peer, 1, pl.ds(0, mper - 1)], outs[s].at[at], (half - 1 - plane, peer),
-            send_f.at[s, 1, step - 1], recv_f.at[s, mirror], start,
-        )
-        first = turn == 0
-        to = jnp.where(first, half - plane, half - 1 - plane)
-        slot = jnp.where(first, 0, near - turn)
-
-        @pl.when(block_id > 0)
-        def _():
-            ship(
-                held.at[s, peer, 1, pl.ds(mper - 1, 1)], outs[s].at[pl.ds(slot * mper, 1)], (to, peer),
-                send_1.at[s, step - 1], recv_1.at[s, slot], start,
-            )
-
-    def e_ship(s, step, start):
-        peer = lax.rem(z + step, gy)
-        ship(
-            held_x.at[s, peer], outs[s].at[pl.ds(0, 1)], (0, peer),
-            send_e.at[s, step - 1], recv_1.at[s, 0], start,
-        )
 
     def fill_x(m, row):
         low = lax.broadcasted_iota(jnp.int32, m.shape, 1)
@@ -621,17 +527,121 @@
             both = jnp.concatenate([re, im], 0).astype(jnp.bfloat16)
             x_tab[pl.ds(row, 2 * m.shape[0]), block * LANES : (block + 1) * LANES] = both
 
-    def build_x():
-        row = lax.broadcasted_iota(jnp.int32, (mper, LANES), 0)
-
-        def body(t, carry):
-            fill_x(row + t * mper, pl.multiple_of(t * own, own))
-            return carry
-
-        lax.fori_loop(0, owners, body, 0)
-        fill_x(jnp.full((8, LANES), NA // 2, jnp.int32), owners * own)
-
-    def build_y():
+    row = lax.broadcasted_iota(jnp.int32, (mper, LANES), 0)
+
+    def body(t, carry):
+        fill_x(row + t * mper, pl.multiple_of(t * own, own))
+        return carry
+
+    lax.fori_loop(0, owners, body, 0)
+    fill_x(jnp.full((8, LANES), NA // 2, jnp.int32), owners * own)
+
+
+def far_kernel(grid_rows, grid_cols, plan, freqs, *rest):
+    sets, each, per = plan
+    sd, outs, rest = rest[:sets], rest[sets : 2 * sets], rest[2 * sets :]
+    x_tab, y_tab, v, g, left, left_x, held, held_x, *sems = rest
+    send_v, recv_v, send_g, recv_g, send_x, recv_x, send_f, recv_f, send_e = sems
+    gx, gy = lax.axis_size("gx"), lax.axis_size("gy")
+    i, z = lax.axis_index("gx"), lax.axis_index("gy")
+    me = i * gy + z
+    count = gx * gy
+    rows = grid_rows // gx
+    cols = grid_cols // gy
+    split = 2 * each // per
+    slabs = cols // LANES
+    mper, owners, near = layout(gx, gy)
+    own = 2 * mper
+    vb = NA // gy
+    wide = NF * each * 2
+    half = gx // 2
+    mesh_id = pl.DeviceIdType.MESH
+
+    upper = i >= half
+    plane = jnp.where(upper, i - half, half - 1 - i)
+    turn = jnp.where(upper, 0, gy) + z
+    block_id = plane * near + turn
+
+    def owner(t):
+        c, r = lax.div(t, near), lax.rem(t, near)
+        return jnp.where(r < gy, half + c, half - 1 - c), lax.rem(r, gy)
+
+    end_i, end_z = owner(jnp.int32(owners - 1))
+
+    def ship(src, dst, where, send_sem, recv_sem):
+        here = (where[0] == i) & (where[1] == z)
+
+        @pl.when(~here)
+        def _():
+            pltpu.make_async_remote_copy(
+                src_ref=src, dst_ref=dst, send_sem=send_sem, recv_sem=recv_sem,
+                device_id=where, device_id_type=mesh_id,
+            ).start()
+
+        @pl.when(here)
+        def _():
+            pltpu.make_async_copy(src, dst, recv_sem).start()
+
+    def wait(ref, sem):
+        pltpu.make_async_copy(ref, ref, sem).wait()
+
+    here = pl.ds(pl.multiple_of(i * rows, rows), rows)
+    lane = pl.multiple_of((z * slabs + lax.div(i, split)) * LANES, LANES)
+    to = (pl.ds(lax.rem(i, split) * per, per), slice(None), pl.ds(lane, LANES))
+
+    def v_ship(s, offset):
+        peer = lax.rem(i + offset, gx)
+        ship(sd[s].at[peer], v.at[s, here], (peer, z), send_v.at[s], recv_v.at[s])
+
+    def g_ship(s, t):
+        part = g.at[s, :, pl.ds(pl.multiple_of(t * own, own), own), :]
+        ship(part, left.at[(s, *to)], owner(t), send_g.at[s], recv_g.at[s])
+
+    def x_ship(s):
+        part = g.at[s, :, pl.ds(owners * own, 16), :]
+        ship(part, left_x.at[(s, *to)], (end_i, end_z), send_x.at[s], recv_x.at[s])
+
+    def held_at(peer, sign):
+        return (peer * 2 + sign) * mper
+
+    def f_ship(s, peer):
+        at = pl.ds(pl.multiple_of(turn * mper, mper), mper)
+        src = held.at[s, pl.ds(held_at(peer, 0), mper)]
+        ship(src, outs[s].at[at], (half + plane, peer), send_f.at[s], recv_f.at[s])
+        at = pl.ds((near - 1 - turn) * mper + 1, mper - 1)
+        src = held.at[s, pl.ds(held_at(peer, 1), mper - 1)]
+        ship(src, outs[s].at[at], (half - 1 - plane, peer), send_f.at[s], recv_f.at[s])
+        first = turn == 0
+        across = jnp.where(first, half - plane, half - 1 - plane)
+        slot = jnp.where(first, 0, near - turn)
+
+        @pl.when(block_id > 0)
+        def _():
+            src = held.at[s, pl.ds(held_at(peer, 1) + mper - 1, 1)]
+            ship(src, outs[s].at[pl.ds(slot * mper, 1)], (across, peer), send_f.at[s], recv_f.at[s])
+
+    def f_sent(s):
+        far_up = (gy - 1) * mper + gy * (mper - 1)
+        far_low = gy * mper + (gy - 1) * mper
+        for case, amount in (
+            (upper & (block_id > 0), far_up + gy), (upper & (block_id == 0), far_up), (~upper, far_low),
+        ):
+
+            @pl.when(case)
+            def _():
+                wait(held.at[s, pl.ds(0, amount)], send_f.at[s])
+
+    def e_ship(s, peer):
+        ship(held_x.at[s, peer], outs[s].at[pl.ds(0, 1)], (0, peer), send_e.at[s], recv_f.at[s])
+
+    def e_sent(s):
+        for case, amount in ((i == 0, gy - 1), (i > 0, gy)):
+
+            @pl.when(case)
+            def _():
+                wait(held_x.at[s, pl.ds(0, amount)], send_e.at[s])
+
+    def build_y(low_block, high_block):
         tall = 32
         low = lax.broadcasted_iota(jnp.int32, (tall, LANES), 1)
         row = lax.broadcasted_iota(jnp.int32, (tall, LANES), 0)
@@ -648,7 +658,7 @@
                 y_tab[1, pl.ds(start, tall), at] = (h_re * b_im + h_im * b_re).astype(jnp.bfloat16)
             return carry
 
-        lax.fori_loop(0, grid_cols // tall, body, 0)
+        lax.fori_loop(grid_cols * low_block // (tall * Y_STEPS), grid_cols * high_block // (tall * Y_STEPS), body, 0)
 
     inv_norm = 1.0 / math.sqrt(grid_rows * grid_cols)
     mix = []
@@ -664,8 +674,7 @@
     group = owners // parts
 
     def transform_rows(s):
-        for src in range(gx):
-            arrived(v.at[s, pl.ds(src * rows, rows)], recv_v.at[s, src])
+        wait(v.at[s], recv_v.at[s])
 
         def body(c, carry):
             chunk = lax.rem(lax.div(block_id, group) + 1 + c, parts)
@@ -679,10 +688,10 @@
             def _():
                 for f in range(per):
                     g[s, f, owners * own :, :] = both[tall:, f * LANES : (f + 1) * LANES]
-                x_ship(s, True)
+                x_ship(s)
 
             for e in range(group):
-                g_ship(s, chunk * group + e, True)
+                g_ship(s, chunk * group + e)
             return carry
 
         lax.fori_loop(0, parts, body, 0)
@@ -708,46 +717,38 @@
             a_re, a_im, b_re, b_im = p_re[top], p_im[top], p_re[low], p_im[low]
             return (a_re - b_im, a_im + b_re), (a_re + b_im, a_im - b_re)
 
-        fields = [both_signs(f) for f in range(2 * EACH)]
+        fields = [both_signs(f) for f in range(2 * each)]
         for f in range(NF):
             p0, p1, q0, q1 = mix[f]
-            for k in range(EACH):
+            for k in range(each):
                 for sign, result in enumerate((plus, minus)):
                     s_re, s_im = fields[k][sign]
-                    d_re, d_im = fields[EACH + k][sign]
+                    d_re, d_im = fields[each + k][sign]
                     result.append(p0 * s_re - p1 * s_im + (q0 * d_re - q1 * d_im))
                     result.append(p0 * s_im + p1 * s_re + (q0 * d_im + q1 * d_re))
         pack = lambda result: jnp.concatenate(result, 0).astype(jnp.bfloat16)
         return pack(plus), pack(minus)
 
     def transform_cols(s):
-        for src in range(count):
-            src_i, src_z = divmod(src, gy)
-            lane = (src_z * slabs + src_i // split) * LANES
-            region = left.at[s, pl.ds(src_i % split * per, per), :, pl.ds(lane, LANES)]
-            arrived(region, recv_g.at[s, src])
-        lhs = left[s].reshape(2 * EACH * own, grid_cols)
+        wait(left.at[s], recv_g.at[s])
+        lhs = left[s].reshape(2 * each * own, grid_cols)
         for step in range(1, gy + 1):
             peer = lax.rem(z + step, gy)
             plus, minus = finish(lhs, mper, peer)
-            held[s, peer, 0] = dot(forth, plus).reshape(mper, wide, vb).astype(jnp.bfloat16)
-            held[s, peer, 1] = dot(back, minus).reshape(mper, wide, vb).astype(jnp.bfloat16)
-            f_ship(s, step, True)
+            held[s, pl.ds(held_at(peer, 0), mper)] = dot(forth, plus).reshape(mper, wide, vb).astype(jnp.bfloat16)
+            held[s, pl.ds(held_at(peer, 1), mper)] = dot(back, minus).reshape(mper, wide, vb).astype(jnp.bfloat16)
+            f_ship(s, peer)
 
     at_end = (i == end_i) & (z == end_z)
 
     def transform_end(s):
-        for src in range(count):
-            src_i, src_z = divmod(src, gy)
-            lane = (src_z * slabs + src_i // split) * LANES
-            region = left_x.at[s, pl.ds(src_i % split * per, per), :, pl.ds(lane, LANES)]
-            arrived(region, recv_x.at[s, src])
-        lhs = left_x[s].reshape(2 * EACH * 16, grid_cols)
+        wait(left_x.at[s], recv_x.at[s])
+        lhs = left_x[s].reshape(2 * each * 16, grid_cols)
         for step in range(1, gy + 1):
             peer = lax.rem(z + step, gy)
             _, minus = finish(lhs, 8, peer)
             held_x[s, peer] = dot(only, minus).reshape(1, wide, vb).astype(jnp.bfloat16)
-            e_ship(s, step, True)
+            e_ship(s, peer)
 
     def owned(body):
         if near == 2 * gy:
@@ -755,57 +756,56 @@
         else:
             pl.when(turn < near)(body)
 
-    for s in range(SETS):
+    barrier = pltpu.get_barrier_semaphore()
+    for offset in range(1, count):
+        peer = lax.rem(me + offset, count)
+        pl.semaphore_signal(
+            barrier, inc=1, device_id=(lax.div(peer, gy), lax.rem(peer, gy)), device_id_type=mesh_id
+        )
+    build_y(0, Y_EARLY)
+    pl.semaphore_wait(barrier, count - 1)
+
+    def send_fields(s):
         for offset in range(gx):
-            v_ship(s, offset, True)
-    build_x()
-    transform_rows(0)
-    build_y()
-    for s in range(1, SETS):
-        transform_rows(s)
-    for s in range(SETS):
+            v_ship(s, offset)
+
+    def do_cols(s):
         owned(functools.partial(transform_cols, s))
         pl.when(at_end)(functools.partial(transform_end, s))
-    for s in range(SETS):
-
-        @pl.when(upper)
+
+    steps = {"a": send_fields, "y": lambda part: build_y(part, part + 1), "r": transform_rows, "x": lambda _: build_x(x_tab, mper, owners), "c": do_cols}
+    for token in ORDER[sets]:
+        steps[token[0]](int(token[1:]))
+    for s in range(sets):
+        wait(outs[s], recv_f.at[s])
+    for s in range(sets):
+        wait(v.at[s, pl.ds(0, (gx - 1) * rows)], send_v.at[s])
+        if near == 2 * gy:
+            wait(g.at[s, :, pl.ds(0, (owners - 1) * own), :], send_g.at[s])
+        else:
+            for case, amount in ((turn < near, owners - 1), (turn >= near, owners)):
+
+                @pl.when(case)
+                def _():
+                    wait(g.at[s, :, pl.ds(0, amount * own), :], send_g.at[s])
+
+        @pl.when(~at_end)
         def _():
-            for slot in range(near):
-                arrived(outs[s].at[pl.ds(slot * mper, mper)], recv_f.at[s, slot])
-
-        @pl.when(~upper)
-        def _():
-            for slot in range(near):
-                arrived(outs[s].at[pl.ds(slot * mper + 1, mper - 1)], recv_f.at[s, slot])
-                arrived(outs[s].at[pl.ds(slot * mper, 1)], recv_1.at[s, slot])
-
-    for s in range(SETS):
-        for offset in range(gx):
-            v_ship(s, offset, False)
-        x_ship(s, False)
-        for t in range(owners):
-            g_ship(s, jnp.int32(t), False)
-
-        def sent():
-            for step in range(1, gy + 1):
-                f_ship(s, step, False)
-
-        owned(sent)
-
-        @pl.when(at_end)
-        def _():
-            for step in range(1, gy + 1):
-                e_ship(s, step, False)
+            wait(g.at[s, :, pl.ds(0, 16), :], send_x.at[s])
+
+        owned(functools.partial(f_sent, s))
+        pl.when(at_end)(functools.partial(e_sent, s))
 
 
 def order_kernel(*refs):
     *parts, out = refs
+    sets, each = len(parts), 4 // len(parts)
     for s, part in enumerate(parts):
         block = part[...].astype(jnp.float32)
         for f in range(NF):
-            for k in range(EACH):
-                at = 2 * (f * EACH + k)
-                out[:, f * 4 + s * EACH + k] = block[:, at : at + 2]
+            for k in range(each):
+                at = 2 * (f * each + k)
+                out[:, f * 4 + s * each + k] = block[:, at : at + 2]
 
 
 def far(sd, freqs, grid_rows, grid_cols):
@@ -814,35 +814,26 @@
     nu, vb = NA // gx, NA // gy
     mper, owners, near = layout(gx, gy)
     lanes = sd[0].shape[2]
-    wide = NF * EACH * 2
+    sets, each, per = split_sets(gx, grid_cols // gy)
+    wide = NF * each * 2
     bf16 = jnp.bfloat16
     dma = pltpu.SemaphoreType.DMA
     done = pl.pallas_call(
-        functools.partial(far_kernel, grid_rows, grid_cols),
-        out_shape=(jax.ShapeDtypeStruct((nu, wide, vb), bf16),) * SETS,
-        in_specs=[SM] + [ANY] * SETS,
-        out_specs=(ANY,) * SETS,
+        functools.partial(far_kernel, grid_rows, grid_cols, (sets, each, per)),
+        out_shape=(jax.ShapeDtypeStruct((nu, wide, vb), bf16),) * sets,
+        in_specs=[SM] + [ANY] * sets,
+        out_specs=(ANY,) * sets,
         scratch_shapes=[
             pltpu.VMEM((NA + 16, grid_rows), bf16),
             pltpu.VMEM((2, grid_cols, NA), bf16),
-            pltpu.VMEM((SETS, grid_rows, lanes), bf16),
-            pltpu.VMEM((SETS, lanes // LANES, NA + 16, LANES), bf16),
-            pltpu.VMEM((SETS, 2 * EACH, 2 * mper, grid_cols), bf16),
-            pltpu.VMEM((SETS, 2 * EACH, 16, grid_cols), bf16),
-            pltpu.VMEM((SETS, gy, 2, mper, wide, vb), bf16),
-            pltpu.VMEM((SETS, gy, 1, wide, vb), bf16),
-            dma((SETS, gx)),
-            dma((SETS, gx)),
-            dma((SETS, owners)),
-            dma((SETS, count)),
-            dma((SETS,)),
-            dma((SETS, count)),
-            dma((SETS, 2, gy)),
-            dma((SETS, near)),
-            dma((SETS, gy)),
-            dma((SETS, near)),
-            dma((SETS, gy)),
-        ],
+            pltpu.VMEM((sets, grid_rows, lanes), bf16),
+            pltpu.VMEM((sets, lanes // LANES, NA + 16, LANES), bf16),
+            pltpu.VMEM((sets, 2 * each, 2 * mper, grid_cols), bf16),
+            pltpu.VMEM((sets, 2 * each, 16, grid_cols), bf16),
+            pltpu.VMEM((sets, gy * 2 * mper, wide, vb), bf16),
+            pltpu.VMEM((sets, gy, 1, wide, vb), bf16),
+        ]
+        + [dma((sets,))] * 9,
         compiler_params=pltpu.CompilerParams(
             vmem_limit_bytes=BIG, collective_id=1, has_side_effects=True
         ),
@@ -853,7 +844,7 @@
         order_kernel,
         grid=(4,),
         out_shape=jax.ShapeDtypeStruct((nu, NF * 4, 2, vb), jnp.float32),
-        in_specs=[pl.BlockSpec((block, wide, vb), lambda n: (n, 0, 0))] * SETS,
+        in_specs=[pl.BlockSpec((block, wide, vb), lambda n: (n, 0, 0))] * sets,
         out_specs=pl.BlockSpec((block, NF * 4, 2, vb), lambda n: (n, 0, 0, 0)),
         name="order",
     )(*done)

time: 106 us -> 99.4 us (0.938)
  Pallas kernels: 105 us -> 98.4 us
    pallas_call x2, Pallas kernels: 88.9 us -> 82 us  [the longest x1 66.2 us: far(): pl.pallas_call(functools.partial(far_kernel, grid_rows, grid_cols, (sets,...]
where the time goes in v6:
time: 99.4 us; the launch traced here: 99 us
  Pallas kernels  98.4 us (99%)
    pallas_call x1, Pallas kernels, far(): pl.pallas_call(functools.partial(far_kernel, grid_rows, grid_cols, (sets,...  66.2 us
    pallas_call x1, Pallas kernels, yee(): pl.pallas_call(functools.partial(yee_kernel, grid_rows, grid_cols, (sets,...  15.9 us
    pallas_call x1, Pallas kernels, halo(): pl.pallas_call(halo_kernel, out_shape=(jax.ShapeDtypeStruct((rows, LANES)...  12.7 us
    pallas_call x1, Pallas kernels, far(): pl.pallas_call(order_kernel, grid=(4,), out_shape=jax.ShapeDtypeStruct((n...  3.67 us

profile of v6, /device:TPU:0, one launch (start us, length us, event | category | flops | bytes accessed | tf_op | source)
XLA Modules:
  0.0 99.0 jit_solution(8893617658245182023)
XLA Ops:
  0.6 12.7 %halo.1 = (f32[256,128]{1,0:T(8,128)}, f32[2,8,128]{2,1,0:T(8,128)}, f32[2,18,8,512]{3,2,1,0:T(8,128)}, s32[2,3,8,512]{3,2,1,0:T(8,128)}) custom-call(f32[9,256,512]{2,1,0:T(8,128)} %bitcast.6, f32[9,256,512]{2,1,0:T(8,128)} %bitcast.8, s32[3,256,512]{2,1,0:T(8,128)} %m_hbm.1), custom_call_target="tpu_custom_call" | custom-call | tf_op jit(solution)/shard_map/halo/pallas_call | solution.py:163
  13.3 15.9 %yee.1 = (f32[9,256,512]{2,1,0:T(8,128)}, f32[9,256,512]{2,1,0:T(8,128)}, bf16[8,256,128]{2,1,0:T(8,128)(2,1)}, bf16[8,256,128]{2,1,0:T(8,128)(2,1)}, bf16[8,256...) custom-call(f32[9,256,512]{2,1,0:T(8,128)} %bitcast.7, f32[9,256,512]{2,1,0:T(8,128)} %bitcast.9, s32[3,256,512]{2,1,0:T(8,128)} %m_hbm.1, ...), custom_call_target="tpu_custom_call" | custom-call | tf_op jit(solution)/shard_map/yee/pallas_call | solution.py:454
  29.2 66.2 %far.1 = (bf16[128,4,256]{2,1,0:T(4,128)(2,1)}, bf16[128,4,256]{2,1,0:T(4,128)(2,1)}, bf16[128,4,256]{2,1,0:T(4,128)(2,1)}, bf16[128,4,256]{2,1,0:T(4,128)(2,1)}) custom-call(f32[2]{0:T(128)} %freqs.1, bf16[8,256,128]{2,1,0:T(8,128)(2,1)} %get-tuple-element.23.rest_0_, bf16[8,256,128]{2,1,0:T(8,128)(2,1)} %get-tuple-element.24.rest_1_, ...), custom_call_target="tpu_custom_call" | custom-call | tf_op jit(solution)/shard_map/far/pallas_call | solution.py:821
  95.4 3.7 %order.1 = f32[128,8,2,256]{3,2,1,0:T(2,128)} custom-call(bf16[128,4,256]{2,1,0:T(4,128)(2,1)} %get-tuple-element.27.refs_0_, bf16[128,4,256]{2,1,0:T(4,128)(2,1)} %get-tuple-element.28.refs_1_, bf16[128,4,256]{2,1,0:T(4,128)(2,1)} %get-tuple-element.29.refs_2_, bf16[128,4,256]{2,1,0:T(4,128)(2,1)} %get-tuple-element.30.refs_3_), custom_call_target="tpu_custom_call" | custom-call | tf_op jit(solution)/shard_map/order/pallas_call | solution.py:843

commit v7 on v6

--- a/solution.py
+++ b/solution.py
@@ -102,27 +102,27 @@
                 copy.start()
 
     start(rows_out)
-    for copy in loads:
-        copy.wait()
     tall = 32
     lane = lax.broadcasted_iota(jnp.int32, (tall, LANES), 1)
 
-    def pack(c, carry):
+    def pack(side, c, carry):
         at = pl.ds(pl.multiple_of(c * tall, tall), tall)
-        for side in range(2):
-            place = ((lane + 2 * side) & (LANES - 1)) >> 2
-            block = jnp.zeros((tall, LANES), jnp.float32)
-            for p in range(2 * planes + LZ):
-                if p < 2 * planes:
-                    piece = edge_f[side, p, at, :]
-                else:
-                    piece = edge_m[side, p - 2 * planes, at, :].astype(jnp.float32)
-                block = jnp.where(place == p, pltpu.roll(piece, 4 * p, 1), block)
-            packed[side, at, :] = block
+        place = ((lane + 2 * side) & (LANES - 1)) >> 2
+        block = jnp.zeros((tall, LANES), jnp.float32)
+        for p in range(2 * planes + LZ):
+            if p < 2 * planes:
+                piece = edge_f[side, p, at, :]
+            else:
+                piece = edge_m[side, p - 2 * planes, at, :].astype(jnp.float32)
+            block = jnp.where(place == p, pltpu.roll(piece, 4 * p, 1), block)
+        packed[side, at, :] = block
         return carry
 
-    lax.fori_loop(0, rows // tall, pack, 0)
-    start(cols_out)
+    for side in range(2):
+        for copy in loads[3 * side : 3 * side + 3]:
+            copy.wait()
+        lax.fori_loop(0, rows // tall, functools.partial(pack, side), 0)
+        start(cols_out[3 * side : 3 * side + 3])
     for step, copy in rows_out + cols_out:
 
         @pl.when(exists((-step[0], -step[1])))
@@ -839,10 +839,10 @@
         ),
         name="far",
     )(freqs, *sd)
-    block = nu // 4
+    block = nu // 1
     return pl.pallas_call(
         order_kernel,
-        grid=(4,),
+        grid=(1,),
         out_shape=jax.ShapeDtypeStruct((nu, NF * 4, 2, vb), jnp.float32),
         in_specs=[pl.BlockSpec((block, wide, vb), lambda n: (n, 0, 0))] * sets,
         out_specs=pl.BlockSpec((block, NF * 4, 2, vb), lambda n: (n, 0, 0, 0)),

time: 99.4 us -> 99.7 us (level)
    pallas_call x1, Pallas kernels: 66.2 us -> 68.2 us  [far(): pl.pallas_call(functools.partial(far_kernel, grid_rows, grid_cols, (sets,...]
where the time goes in v7:
time: 99.7 us; the launch traced here: 99.6 us
  Pallas kernels  98.9 us (99%)
    pallas_call x1, Pallas kernels, far(): pl.pallas_call(functools.partial(far_kernel, grid_rows, grid_cols, (sets,...  68.2 us
    pallas_call x1, Pallas kernels, yee(): pl.pallas_call(functools.partial(yee_kernel, grid_rows, grid_cols, (sets,...  15.9 us
    pallas_call x1, Pallas kernels, halo(): pl.pallas_call(halo_kernel, out_shape=(jax.ShapeDtypeStruct((rows, LANES)...  11.8 us
    pallas_call x1, Pallas kernels, far(): pl.pallas_call(order_kernel, grid=(1,), out_shape=jax.ShapeDtypeStruct((n...  3.09 us

profile of v7, /device:TPU:0, one launch (start us, length us, event | category | flops | bytes accessed | tf_op | source)
XLA Modules:
  0.0 99.6 jit_solution(14213420655099535504)
XLA Ops:
  0.6 11.8 %halo.1 = (f32[256,128]{1,0:T(8,128)}, f32[2,8,128]{2,1,0:T(8,128)}, f32[2,18,8,512]{3,2,1,0:T(8,128)}, s32[2,3,8,512]{3,2,1,0:T(8,128)}) custom-call(f32[9,256,512]{2,1,0:T(8,128)} %bitcast.6, f32[9,256,512]{2,1,0:T(8,128)} %bitcast.8, s32[3,256,512]{2,1,0:T(8,128)} %m_hbm.1), custom_call_target="tpu_custom_call" | custom-call | tf_op jit(solution)/shard_map/halo/pallas_call | solution.py:163
  12.4 15.9 %yee.1 = (f32[9,256,512]{2,1,0:T(8,128)}, f32[9,256,512]{2,1,0:T(8,128)}, bf16[8,256,128]{2,1,0:T(8,128)(2,1)}, bf16[8,256,128]{2,1,0:T(8,128)(2,1)}, bf16[8,256...) custom-call(f32[9,256,512]{2,1,0:T(8,128)} %bitcast.7, f32[9,256,512]{2,1,0:T(8,128)} %bitcast.9, s32[3,256,512]{2,1,0:T(8,128)} %m_hbm.1, ...), custom_call_target="tpu_custom_call" | custom-call | tf_op jit(solution)/shard_map/yee/pallas_call | solution.py:454
  28.3 68.2 %far.1 = (bf16[128,4,256]{2,1,0:T(4,128)(2,1)}, bf16[128,4,256]{2,1,0:T(4,128)(2,1)}, bf16[128,4,256]{2,1,0:T(4,128)(2,1)}, bf16[128,4,256]{2,1,0:T(4,128)(2,1)}) custom-call(f32[2]{0:T(128)} %freqs.1, bf16[8,256,128]{2,1,0:T(8,128)(2,1)} %get-tuple-element.23.rest_0_, bf16[8,256,128]{2,1,0:T(8,128)(2,1)} %get-tuple-element.24.rest_1_, ...), custom_call_target="tpu_custom_call" | custom-call | tf_op jit(solution)/shard_map/far/pallas_call | solution.py:821
  96.5 3.1 %order.1 = f32[128,8,2,256]{3,2,1,0:T(2,128)} custom-call(bf16[128,4,256]{2,1,0:T(4,128)(2,1)} %get-tuple-element.27.refs_0_, bf16[128,4,256]{2,1,0:T(4,128)(2,1)} %get-tuple-element.28.refs_1_, bf16[128,4,256]{2,1,0:T(4,128)(2,1)} %get-tuple-element.29.refs_2_, bf16[128,4,256]{2,1,0:T(4,128)(2,1)} %get-tuple-element.30.refs_3_), custom_call_target="tpu_custom_call" | custom-call | tf_op jit(solution)/shard_map/order/pallas_call | solution.py:843

commit v8 on v6

--- a/solution.py
+++ b/solution.py
@@ -839,10 +839,10 @@
         ),
         name="far",
     )(freqs, *sd)
-    block = nu // 4
+    block = nu
     return pl.pallas_call(
         order_kernel,
-        grid=(4,),
+        grid=(1,),
         out_shape=jax.ShapeDtypeStruct((nu, NF * 4, 2, vb), jnp.float32),
         in_specs=[pl.BlockSpec((block, wide, vb), lambda n: (n, 0, 0))] * sets,
         out_specs=pl.BlockSpec((block, NF * 4, 2, vb), lambda n: (n, 0, 0, 0)),

time: 99.4 us -> 98.6 us (level)
  no operation moved by 1% of the time
where the time goes in v8:
time: 98.6 us; the launch traced here: 98.4 us
  Pallas kernels  97.8 us (99%)
    pallas_call x1, Pallas kernels, far(): pl.pallas_call(functools.partial(far_kernel, grid_rows, grid_cols, (sets,...  66.2 us
    pallas_call x1, Pallas kernels, yee(): pl.pallas_call(functools.partial(yee_kernel, grid_rows, grid_cols, (sets,...  15.9 us
    pallas_call x1, Pallas kernels, halo(): pl.pallas_call(halo_kernel, out_shape=(jax.ShapeDtypeStruct((rows, LANES)...  12.7 us
    pallas_call x1, Pallas kernels, far(): pl.pallas_call(order_kernel, grid=(1,), out_shape=jax.ShapeDtypeStruct((n...  3.09 us

profile of v8, /device:TPU:0, one launch (start us, length us, event | category | flops | bytes accessed | tf_op | source)
XLA Modules:
  0.0 98.4 jit_solution(14747286145740669809)
XLA Ops:
  0.6 12.7 %halo.1 = (f32[256,128]{1,0:T(8,128)}, f32[2,8,128]{2,1,0:T(8,128)}, f32[2,18,8,512]{3,2,1,0:T(8,128)}, s32[2,3,8,512]{3,2,1,0:T(8,128)}) custom-call(f32[9,256,512]{2,1,0:T(8,128)} %bitcast.6, f32[9,256,512]{2,1,0:T(8,128)} %bitcast.8, s32[3,256,512]{2,1,0:T(8,128)} %m_hbm.1), custom_call_target="tpu_custom_call" | custom-call | tf_op jit(solution)/shard_map/halo/pallas_call | solution.py:163
  13.3 15.9 %yee.1 = (f32[9,256,512]{2,1,0:T(8,128)}, f32[9,256,512]{2,1,0:T(8,128)}, bf16[8,256,128]{2,1,0:T(8,128)(2,1)}, bf16[8,256,128]{2,1,0:T(8,128)(2,1)}, bf16[8,256...) custom-call(f32[9,256,512]{2,1,0:T(8,128)} %bitcast.7, f32[9,256,512]{2,1,0:T(8,128)} %bitcast.9, s32[3,256,512]{2,1,0:T(8,128)} %m_hbm.1, ...), custom_call_target="tpu_custom_call" | custom-call | tf_op jit(solution)/shard_map/yee/pallas_call | solution.py:454
  29.2 66.2 %far.1 = (bf16[128,4,256]{2,1,0:T(4,128)(2,1)}, bf16[128,4,256]{2,1,0:T(4,128)(2,1)}, bf16[128,4,256]{2,1,0:T(4,128)(2,1)}, bf16[128,4,256]{2,1,0:T(4,128)(2,1)}) custom-call(f32[2]{0:T(128)} %freqs.1, bf16[8,256,128]{2,1,0:T(8,128)(2,1)} %get-tuple-element.23.rest_0_, bf16[8,256,128]{2,1,0:T(8,128)(2,1)} %get-tuple-element.24.rest_1_, ...), custom_call_target="tpu_custom_call" | custom-call | tf_op jit(solution)/shard_map/far/pallas_call | solution.py:821
  95.4 3.1 %order.1 = f32[128,8,2,256]{3,2,1,0:T(2,128)} custom-call(bf16[128,4,256]{2,1,0:T(4,128)(2,1)} %get-tuple-element.27.refs_0_, bf16[128,4,256]{2,1,0:T(4,128)(2,1)} %get-tuple-element.28.refs_1_, bf16[128,4,256]{2,1,0:T(4,128)(2,1)} %get-tuple-element.29.refs_2_, bf16[128,4,256]{2,1,0:T(4,128)(2,1)} %get-tuple-element.30.refs_3_), custom_call_target="tpu_custom_call" | custom-call | tf_op jit(solution)/shard_map/order/pallas_call | solution.py:843
